TPU v7x, 32 devices: a whole 2x2x4 slice. The times are simulated.
32 devices in a mesh: row: 4 (over y, x), col: 8 (over z, core).
Axes of the slice: x: 2, y: 2, z: 4, core: 2. Of those that a mesh axis runs over, the one named last changes fastest.
Arguments:
- latent: bfloat16 [128, 256, 512], P('row', 'col'), may hold values from -12 to 12
- conv_scale: float32 [512], replicated, may hold values from 0.5 to 1.5
- conv_shift: float32 [512], replicated, may hold values from -3 to 3
- expand_weight: bfloat16 [512, 2048], replicated, may hold values from -0.25 to 0.25
- depth_kernel: float32 [9, 2048], replicated, may hold values from -2 to 2
- squeeze_down: bfloat16 [2048, 128], replicated, may hold values from -0.5 to 0.5
- squeeze_up: bfloat16 [128, 2048], replicated, may hold values from -0.5 to 0.5
- project_weight: bfloat16 [2048, 512], replicated, may hold values from -0.125 to 0.125
- block_gain: float32 [512], replicated, may hold values from 0.5 to 1.5
- block_projection: bfloat16 [512, 1536], replicated, may hold values from -0.25 to 0.25
- block_output: bfloat16 [512, 512], replicated, may hold values from -0.25 to 0.25
- block_table: float32 [16, 225], replicated, may hold values from -4 to 300
- first_gain: float32 [512], replicated, may hold values from 0.5 to 1.5
- first_expand: bfloat16 [512, 2048], replicated, may hold values from -0.25 to 0.25
- first_reduce: bfloat16 [2048, 512], replicated, may hold values from -0.125 to 0.125
- grid_gain: float32 [512], replicated, may hold values from 0.5 to 1.5
- grid_projection: bfloat16 [512, 1536], replicated, may hold values from -0.25 to 0.25
- grid_output: bfloat16 [512, 512], replicated, may hold values from -0.25 to 0.25
- grid_table: float32 [16, 225], replicated, may hold values from -4 to 300
- second_gain: float32 [512], replicated, may hold values from 0.5 to 1.5
- second_expand: bfloat16 [512, 2048], replicated, may hold values from -0.25 to 0.25
- second_reduce: bfloat16 [2048, 512], replicated, may hold values from -0.125 to 0.125
Outputs:
- nowcast_latent: bfloat16 [128, 256, 512], P('row', 'col')
All inputs are finite; a program needn't handle non-finite values.
Results may differ from a plain program's by a relative error of at most 0.012.
Values may be sent and summed in bfloat16 or wider, within the bound.
A program may use at most 128 MiB of HBM per device.

v0:
```python
import functools

import jax
import jax.numpy as jnp
import numpy as np
from jax import lax
from jax.experimental import pallas as pl
from jax.experimental.pallas import tpu as pltpu
from jax.sharding import PartitionSpec as P

WIN = 8


def extended(cells, sides, width):
    for axis, dim in sides:
        count = lax.axis_size(axis)
        ends = count - 1
        head = lax.slice_in_dim(cells, 0, width, axis=dim)
        tail = lax.slice_in_dim(cells, cells.shape[dim] - width, cells.shape[dim], axis=dim)
        cells = jnp.concatenate(
            [
                lax.ppermute(tail, axis, [(i, (i + 1) % count) for i in range(ends)]),
                cells,
                lax.ppermute(head, axis, [((i + 1) % count, i) for i in range(ends)]),
            ],
            axis=dim,
        )
    return cells


def layer_norm_apply(values, norm_gain):
    widened = values.astype(jnp.float32)
    center = widened - jnp.mean(widened, axis=-1, keepdims=True)
    spread = jnp.mean(center * center, axis=-1, keepdims=True)
    return (center * lax.rsqrt(spread + 1e-05) * norm_gain).astype(jnp.bfloat16)


def position_bias(offset_bias_lookup):
    spots = offset_bias_lookup.shape[1]
    position = jnp.arange(WIN * WIN)
    down_pos = position // WIN
    across = position % WIN
    relative = (down_pos[:, None] - down_pos[None, :] + WIN - 1) * (2 * WIN - 1) + (
        across[:, None] - across[None, :] + WIN - 1
    )
    indicator_matrix = (relative[:, :, None] == jnp.arange(spots)[None, None, :]).astype(
        jnp.float32
    )
    return jnp.einsum(
        "bp,rjp->brj", offset_bias_lookup, indicator_matrix, precision=lax.Precision.HIGHEST
    )


def attend(triple, pos_bias):
    window_count, tokens, three_width = triple.shape
    feature_width = three_width // 3
    head_count = pos_bias.shape[0]
    head_size = feature_width // head_count
    queries = triple[..., :feature_width].reshape(window_count, tokens, head_count, head_size)
    key_row_list = triple[..., feature_width : 2 * feature_width].reshape(
        window_count, tokens, head_count, head_size
    )
    values = triple[..., 2 * feature_width :].reshape(window_count, tokens, head_count, head_size)
    scores = (
        jnp.einsum("nqhd,nkhd->nhqk", queries, key_row_list, preferred_element_type=jnp.float32)
        * head_size ** (-0.5)
        + pos_bias[None]
    )
    row_max = jnp.max(scores, axis=-1, keepdims=True)
    weight_tensors = jnp.exp(scores - row_max)
    attention_weight_map = (
        weight_tensors / jnp.sum(weight_tensors, axis=-1, keepdims=True)
    ).astype(jnp.bfloat16)
    mixed = jnp.einsum(
        "nhqk,nkhd->nqhd", attention_weight_map, values, preferred_element_type=jnp.float32
    )
    return mixed.astype(jnp.bfloat16).reshape(window_count, tokens, feature_width)


def attention_sublayer(windows, norm_gain, in_weight, out_weight, pos_bias):
    normed = layer_norm_apply(windows, norm_gain)
    triple = jnp.dot(normed, in_weight, preferred_element_type=jnp.float32).astype(jnp.bfloat16)
    mixed = attend(triple, pos_bias)
    return (
        windows.astype(jnp.float32) + jnp.dot(mixed, out_weight, preferred_element_type=jnp.float32)
    ).astype(jnp.bfloat16)


def feed_forward(values, norm_gain, in_weight, out_weight):
    normed = layer_norm_apply(values, norm_gain)
    hidden = jax.nn.gelu(
        jnp.dot(normed, in_weight, preferred_element_type=jnp.float32), approximate=True
    ).astype(jnp.bfloat16)
    return (
        values.astype(jnp.float32) + jnp.dot(hidden, out_weight, preferred_element_type=jnp.float32)
    ).astype(jnp.bfloat16)


def to_blocks(field):
    row_count, col_count, feats = field.shape
    return (
        field.reshape(row_count // WIN, WIN, col_count // WIN, WIN, feats)
        .transpose(0, 2, 1, 3, 4)
        .reshape(-1, WIN * WIN, feats)
    )


def from_blocks(windows, row_count, col_count):
    feats = windows.shape[-1]
    return (
        windows.reshape(row_count // WIN, col_count // WIN, WIN, WIN, feats)
        .transpose(0, 2, 1, 3, 4)
        .reshape(row_count, col_count, feats)
    )


def axis_shape(length, devices):
    fold = max(1, WIN // devices)
    rest = length // max(devices, WIN)
    span = min(devices, WIN)
    return (fold, rest, span, devices // span)


def grid_layout(field):
    row_devices = lax.axis_size("row")
    col_devices = lax.axis_size("col")
    row_count, col_count, feats = field.shape
    row_fold, row_rest, row_span, row_hop = axis_shape(row_count, row_devices)
    col_fold, col_rest, col_span, col_hop = axis_shape(col_count, col_devices)
    ordered_layout = field.reshape(
        row_fold, row_devices, row_rest, col_fold, col_devices, col_rest, feats
    )
    flat = ordered_layout.transpose(1, 4, 0, 2, 3, 5, 6).reshape(
        row_devices * col_devices, row_fold, row_rest, col_fold, col_rest, feats
    )
    flat = lax.all_to_all(flat, ("row", "col"), split_axis=0, concat_axis=0, tiled=True)
    moved = flat.reshape(
        row_devices, col_devices, row_fold, row_rest, col_fold, col_rest, feats
    ).transpose(2, 0, 3, 4, 1, 5, 6)
    moved = moved.reshape(
        row_fold, row_span, row_hop, row_rest, col_fold, col_span, col_hop, col_rest, feats
    )
    return moved.transpose(2, 3, 6, 7, 1, 0, 5, 4, 8).reshape(-1, WIN * WIN, feats)


def spatial_layout(windows, row_count, col_count):
    row_devices = lax.axis_size("row")
    col_devices = lax.axis_size("col")
    feats = windows.shape[-1]
    row_fold, row_rest, row_span, row_hop = axis_shape(row_count, row_devices)
    col_fold, col_rest, col_span, col_hop = axis_shape(col_count, col_devices)
    gridded = windows.reshape(
        row_hop, row_rest, col_hop, col_rest, row_span, row_fold, col_span, col_fold, feats
    )
    ordered_layout = gridded.transpose(5, 4, 0, 1, 7, 6, 2, 3, 8).reshape(
        row_fold, row_devices, row_rest, col_fold, col_devices, col_rest, feats
    )
    flat = ordered_layout.transpose(1, 4, 0, 2, 3, 5, 6).reshape(
        row_devices * col_devices, row_fold, row_rest, col_fold, col_rest, feats
    )
    flat = lax.all_to_all(flat, ("row", "col"), split_axis=0, concat_axis=0, tiled=True)
    moved = flat.reshape(
        row_devices, col_devices, row_fold, row_rest, col_fold, col_rest, feats
    ).transpose(2, 0, 3, 4, 1, 5, 6)
    return moved.reshape(row_count, col_count, feats)


def squeeze_gate(pooled, squeeze_down, squeeze_up):
    reduced = jax.nn.silu(
        jnp.dot(pooled[None, :], squeeze_down.astype(jnp.float32), precision=lax.Precision.HIGHEST)
    )
    return jax.nn.sigmoid(
        jnp.dot(reduced, squeeze_up.astype(jnp.float32), precision=lax.Precision.HIGHEST)
    )[0]


def axis_sum_kernel(axis, count, x_ref, o_ref, slots, send_sem, recv_sem):
    me = lax.axis_index(axis)
    barrier = pltpu.get_barrier_semaphore()
    peers = [lax.rem(me + step, count) for step in range(1, count)]
    for peer in peers:
        pl.semaphore_signal(
            barrier, inc=1, device_id={axis: peer}, device_id_type=pl.DeviceIdType.MESH
        )
    pl.semaphore_wait(barrier, count - 1)
    copies = []
    for step, peer in enumerate(peers):
        copy = pltpu.make_async_remote_copy(
            src_ref=x_ref,
            dst_ref=slots.at[step],
            send_sem=send_sem.at[step],
            recv_sem=recv_sem.at[step],
            device_id={axis: peer},
            device_id_type=pl.DeviceIdType.MESH,
        )
        copy.start()
        copies.append(copy)
    for copy in copies:
        copy.wait()
    total = x_ref[...]
    for step in range(count - 1):
        total = total + slots[step]
    o_ref[...] = total


def axis_sum(values, axis, collective_id):
    count = lax.axis_size(axis)
    if count == 1:
        return values
    return pl.pallas_call(
        functools.partial(axis_sum_kernel, axis, count),
        out_shape=jax.ShapeDtypeStruct(values.shape, values.dtype),
        in_specs=[pl.BlockSpec(memory_space=pltpu.VMEM)],
        out_specs=pl.BlockSpec(memory_space=pltpu.VMEM),
        scratch_shapes=[
            pltpu.VMEM((count - 1,) + values.shape, values.dtype),
            pltpu.SemaphoreType.DMA((count - 1,)),
            pltpu.SemaphoreType.DMA((count - 1,)),
        ],
        compiler_params=pltpu.CompilerParams(collective_id=collective_id, has_side_effects=True),
        name="axis_sum_" + axis,
    )(values)


LANES = 128
GROUP = 256


def normed_rows(widened, gain):
    center = widened - jnp.mean(widened, axis=-1, keepdims=True)
    spread = jnp.mean(center * center, axis=-1, keepdims=True)
    return (center * lax.rsqrt(spread + 1e-05) * gain).astype(jnp.bfloat16)


def mixer_kernel(
    layout, head_size, x_ref, gain_ref, bias_ref, late_gain_ref, proj_hbm, out_hbm, up_hbm, down_hbm,
    o_ref, triple, heads, proj_ref, out_w_ref, up_ref, down_ref, sems,
):
    kind, across = layout
    rows_total, feats = x_ref.shape
    tokens = WIN * WIN
    window_count = rows_total // tokens
    slabs = feats // LANES
    per_slab = LANES // head_size
    moves = [
        pltpu.make_async_copy(src, dst, sems.at[k])
        for k, (src, dst) in enumerate(
            ((proj_hbm, proj_ref), (out_hbm, out_w_ref), (up_hbm, up_ref), (down_hbm, down_ref))
        )
    ]
    for move in moves:
        move.start()
    moves[0].wait()
    chunk = 256

    def project(step, carry):
        rows = pl.ds(pl.multiple_of(step * chunk, chunk), chunk)
        normed = normed_rows(x_ref[rows, :].astype(jnp.float32), gain_ref[...])
        for part in range(3 * slabs // 2):
            product = jnp.dot(
                normed, proj_ref[:, part * GROUP : (part + 1) * GROUP],
                preferred_element_type=jnp.float32,
            ).astype(jnp.bfloat16).astype(jnp.float32)
            triple[2 * part, rows, :] = product[:, :LANES]
            triple[2 * part + 1, rows, :] = product[:, LANES:]
        return carry

    lax.fori_loop(0, rows_total // chunk, project, 0)

    def places(window):
        if kind == "strided":
            return [pl.ds(window, tokens, stride=across)]
        per_row = across // WIN
        base = (window // per_row) * (WIN * across) + (window % per_row) * WIN
        return [pl.ds(pl.multiple_of(base + r * across, WIN), WIN) for r in range(WIN)]

    lane = lax.broadcasted_iota(jnp.int32, (tokens, GROUP), 1)
    head_of = (lane % LANES) // head_size
    scale = head_size ** (-0.5)

    def one_window(window):
        spots = places(window)

        def fetch(slab):
            pieces = [triple[slab, spot, :] for spot in spots]
            whole = pieces[0] if len(pieces) == 1 else jnp.concatenate(pieces, axis=0)
            return whole

        empty = jnp.zeros((tokens, LANES), jnp.bfloat16)
        for group in range(slabs // 2):
            first, second = 2 * group, 2 * group + 1
            query_0 = fetch(first).astype(jnp.bfloat16)
            query_1 = fetch(second).astype(jnp.bfloat16)
            keys = jnp.concatenate([fetch(slabs + first), fetch(slabs + second)], axis=1)
            vals = jnp.concatenate([fetch(2 * slabs + first), fetch(2 * slabs + second)], axis=1)
            block_q = jnp.concatenate(
                [
                    jnp.concatenate([query_0, empty], axis=1),
                    jnp.concatenate([empty, query_1], axis=1),
                ],
                axis=0,
            )
            block_k = jnp.concatenate(
                [jnp.where(head_of == j, keys, 0.0).astype(jnp.bfloat16) for j in range(per_slab)],
                axis=0,
            )
            block_v = jnp.concatenate(
                [jnp.where(head_of == j, vals, 0.0).astype(jnp.bfloat16) for j in range(per_slab)],
                axis=0,
            )
            scores = lax.dot_general(
                block_k, block_q, (((1,), (1,)), ((), ())), preferred_element_type=jnp.float32
            )
            scores = (scores * scale + bias_ref[group]).reshape(per_slab, tokens, 2 * tokens)
            weights = jnp.exp(scores - jnp.max(scores, axis=1, keepdims=True))
            shares = weights / jnp.sum(weights, axis=1, keepdims=True)
            shares = shares.reshape(per_slab * tokens, 2 * tokens).astype(jnp.bfloat16)
            mixed = lax.dot_general(
                shares, block_v, (((0,), (0,)), ((), ())), preferred_element_type=jnp.float32
            )
            for slab, part in (
                (first, mixed[:tokens, :LANES]), (second, mixed[tokens:, LANES:])
            ):
                if len(spots) == 1:
                    heads[slab, spots[0], :] = part
                else:
                    for r, spot in enumerate(spots):
                        heads[slab, spot, :] = part[r * WIN : (r + 1) * WIN]

    def attend_pair(step, carry):
        one_window(2 * step)
        one_window(2 * step + 1)
        return carry

    lax.fori_loop(0, window_count // 2, attend_pair, 0)
    for move in moves[1:]:
        move.wait()
    hidden_width = up_ref.shape[1]
    tile = 512

    def feed(step, carry):
        rows = pl.ds(pl.multiple_of(step * chunk, chunk), chunk)
        mixed = jnp.concatenate([heads[s, rows, :] for s in range(slabs)], axis=1).astype(jnp.bfloat16)
        value = (
            x_ref[rows, :].astype(jnp.float32)
            + jnp.dot(mixed, out_w_ref[...], preferred_element_type=jnp.float32)
        ).astype(jnp.bfloat16).astype(jnp.float32)
        normed = normed_rows(value, late_gain_ref[...])
        for k in range(hidden_width // tile):
            part = slice(k * tile, (k + 1) * tile)
            hidden = jax.nn.gelu(
                jnp.dot(normed, up_ref[:, part], preferred_element_type=jnp.float32),
                approximate=True,
            ).astype(jnp.bfloat16)
            value = value + jnp.dot(hidden, down_ref[part, :], preferred_element_type=jnp.float32)
        o_ref[rows, :] = value.astype(jnp.bfloat16)
        return carry

    lax.fori_loop(0, rows_total // chunk, feed, 0)


def mixer(x, layout, gain, in_weight, out_weight, bias, late_gain, up, down, heads_count):
    rows, feats = x.shape
    vmem = pl.BlockSpec(memory_space=pltpu.VMEM)
    hbm = pl.BlockSpec(memory_space=pl.ANY)
    flops = 2 * rows * feats * (4 * feats + 2 * up.shape[1])
    return pl.pallas_call(
        functools.partial(mixer_kernel, layout, feats // heads_count),
        out_shape=jax.ShapeDtypeStruct((rows, feats), jnp.bfloat16),
        in_specs=[vmem] * 4 + [hbm] * 4,
        out_specs=vmem,
        scratch_shapes=[
            pltpu.VMEM((3 * feats // LANES, rows, LANES), jnp.float32),
            pltpu.VMEM((feats // LANES, rows, LANES), jnp.float32),
            pltpu.VMEM(in_weight.shape, jnp.bfloat16),
            pltpu.VMEM(out_weight.shape, jnp.bfloat16),
            pltpu.VMEM(up.shape, jnp.bfloat16),
            pltpu.VMEM(down.shape, jnp.bfloat16),
            pltpu.SemaphoreType.DMA((4,)),
        ],
        compiler_params=pltpu.CompilerParams(vmem_limit_bytes=48 * 1024 * 1024),
        cost_estimate=pl.CostEstimate(
            flops=flops, bytes_accessed=12 * 1024 * 1024, transcendentals=0
        ),
        name="mixer_" + layout[0],
    )(x, gain[None], bias, late_gain[None], in_weight, out_weight, up, down)


def key_major_bias(table, down, across):
    head_count, spots = table.shape
    relative = (down[None, :] - down[:, None] + WIN - 1) * (2 * WIN - 1) + (
        across[None, :] - across[:, None] + WIN - 1
    )
    tokens = WIN * WIN
    chosen = (jnp.arange(spots)[:, None] == jnp.asarray(relative.reshape(-1))[None, :]).astype(
        jnp.float32
    )
    spread = jnp.dot(table, chosen, precision=lax.Precision.HIGHEST)
    return (
        spread.reshape(head_count // 8, 2, 4, tokens, tokens)
        .transpose(0, 2, 3, 1, 4)
        .reshape(head_count // 8, 4 * tokens, 2 * tokens)
    )


def grid_sublayers(section, run, grid_table):
    row_devices = lax.axis_size("row")
    col_devices = lax.axis_size("col")
    row_count, col_count, feats = section.shape
    plain = np.arange(WIN * WIN)
    if row_devices > WIN or col_devices > WIN:
        windows = grid_layout(section)
        count = windows.shape[0]
        bias = key_major_bias(grid_table, plain // WIN, plain % WIN)
        out = run(windows.transpose(1, 0, 2).reshape(-1, feats), ("strided", count), bias)
        out = out.reshape(WIN * WIN, count, feats).transpose(1, 0, 2)
        return spatial_layout(out, row_count, col_count)
    devices = row_devices * col_devices
    row_fold, col_fold = WIN // row_devices, WIN // col_devices
    row_rest, col_rest = row_count // row_fold, col_count // col_fold
    count = row_rest * col_rest // devices
    pieces = col_rest // count
    sent = (
        section.reshape(row_fold, row_rest, col_fold, pieces, count, feats)
        .transpose(1, 3, 0, 2, 4, 5)
        .reshape(devices, row_fold * col_fold * count, feats)
    )
    got = lax.all_to_all(sent, ("row", "col"), split_axis=0, concat_axis=0, tiled=True)
    order = np.arange(WIN * WIN).reshape(row_devices, col_devices, row_fold, col_fold)
    at = np.indices(order.shape).reshape(4, -1)
    bias = key_major_bias(grid_table, at[0] * row_fold + at[2], at[1] * col_fold + at[3])
    out = run(got.reshape(-1, feats), ("strided", count), bias)
    back = lax.all_to_all(
        out.reshape(devices, -1, feats), ("row", "col"), split_axis=0, concat_axis=0, tiled=True
    )
    return (
        back.reshape(row_rest, pieces, row_fold, col_fold, count, feats)
        .transpose(2, 0, 3, 1, 4, 5)
        .reshape(row_count, col_count, feats)
    )


def per_device(
    latent,
    conv_scale,
    conv_shift,
    expand_weight,
    depth_kernel,
    squeeze_down,
    squeeze_up,
    project_weight,
    block_gain,
    block_projection,
    block_output,
    block_table,
    first_gain,
    first_expand,
    first_reduce,
    grid_gain,
    grid_projection,
    grid_output,
    grid_table,
    second_gain,
    second_expand,
    second_reduce,
):
    row_devices = lax.axis_size("row")
    col_devices = lax.axis_size("col")
    row_count, col_count, channels = latent.shape
    conv_in = (latent.astype(jnp.float32) * conv_scale + conv_shift).astype(jnp.bfloat16)
    expanded = jax.nn.gelu(
        jnp.dot(conv_in, expand_weight, preferred_element_type=jnp.float32), approximate=True
    ).astype(jnp.bfloat16)
    padded = extended(expanded, (("row", 0), ("col", 1)), 1)
    summed = jnp.zeros((row_count, col_count, padded.shape[-1]), jnp.float32)
    for offset in range(9):
        down_step = offset // 3
        side_step = offset % 3
        summed = (
            summed
            + padded[down_step : down_step + row_count, side_step : side_step + col_count].astype(
                jnp.float32
            )
            * depth_kernel[offset]
        )
    depthwise = jax.nn.gelu(summed, approximate=True)
    local_sums = jnp.sum(depthwise, axis=(0, 1)).reshape(-1, 128)
    channel_sums = axis_sum(axis_sum(local_sums, "row", 1), "col", 2).reshape(-1)
    pooled = channel_sums / (row_count * row_devices * col_count * col_devices)
    excite = squeeze_gate(pooled, squeeze_down, squeeze_up)
    gated = (depthwise * excite).astype(jnp.bfloat16)
    conv_out = (
        latent.astype(jnp.float32)
        + jnp.dot(gated, project_weight, preferred_element_type=jnp.float32)
    ).astype(jnp.bfloat16)
    plain = np.arange(WIN * WIN)
    section = mixer(
        conv_out.reshape(-1, channels), ("blocks", col_count), block_gain, block_projection,
        block_output, key_major_bias(block_table, plain // WIN, plain % WIN), first_gain,
        first_expand, first_reduce, block_table.shape[0],
    ).reshape(row_count, col_count, channels)

    def run(cells, layout, bias):
        return mixer(
            cells, layout, grid_gain, grid_projection, grid_output, bias, second_gain,
            second_expand, second_reduce, grid_table.shape[0],
        )

    return grid_sublayers(section, run, grid_table)


def solution(mesh):
    placed = (
        P("row", "col", None),
        P(),
        P(),
        P(),
        P(),
        P(),
        P(),
        P(),
        P(),
        P(),
        P(),
        P(),
        P(),
        P(),
        P(),
        P(),
        P(),
        P(),
        P(),
        P(),
        P(),
        P(),
    )
    return jax.shard_map(
        per_device, mesh=mesh, in_specs=placed, out_specs=P("row", "col", None), check_vma=False
    )
```

profile of v0, /device:TPU:0, one launch (start us, length us, event | category | flops | bytes accessed | tf_op | source)
XLA Modules:
  0.0 188.1 jit_solution(6483011808847942867)
XLA Ops:
  0.0 0.0 copy-start
  0.0 1.6 copy-done
  1.7 5.2 %fusion.7 = bf16[32,32,2048]{2,1,0:T(8,128)(2,1)S(1)} fusion(bf16[512,2048]{1,0:T(8,128)(2,1)S(1)} %copy-done, bf16[32,32,512]{2,1,0:T(8,128)(2,1)} %param.24, f32[512]{0:T(512)} %param.26, f32[512]{0:T(512)} %param.25), kind=kOutput, calls=%fused_computation.9 | convolution fusion | flops 2168455168 | bytes 7344128 | tf_op jit(solution)/shard_map/dot_general | solution.py:472
  6.9 0.0 copy-start.9
  6.9 4.9 %collective-permute-start = (bf16[1,32,2048]{2,1,0:T(8,128)(2,1)S(1)}, bf16[1,32,2048]{2,1,0:T(8,128)(2,1)S(1)}, u32[]{:S(2)}, u32[]{:S(2)}) collective-permute-start(bf16[1,32,2048]{2,1,0:T(8,128)(2,1)S(1)} %get-tuple-element.11), channel_id=1, source_target_pairs={{0,8},{8,16},{16,24},{1,9},{9,17},{17,25},{2,10},{10,18},{18,26},{... | collective-permute-start | bytes 393224 | tf_op jit(solution)/shard_map/ppermute | solution.py:22
  11.8 1.3 collective-permute-start.1
  13.1 0.0 copy-done.14
  13.1 0.7 fusion.38
  13.8 0.7 collective-permute-done
  14.5 4.8 %collective-permute-done.1 = bf16[1,32,2048]{2,1,0:T(8,128)(2,1)S(1)} collective-permute-done((bf16[1,32,2048]{2,1,0:T(8,128)(2,1)S(1)}, bf16[1,32,2048]{2,1,0:T(8,128)(2,1)S(1)}, u32[]{:S(2)}, u32[]{:S(2)}) %collective-permute-start.1) | collective-permute-done | bytes 131104 | tf_op jit(solution)/shard_map/ppermute | solution.py:24
  19.3 0.0 copy-done.9
  19.3 1.3 pad_maximum_fusion.5
  20.6 2.0 %collective-permute-start.2 = (bf16[34,1,2048]{2,1,0:T(2,128)(2,1)}, bf16[34,1,2048]{2,1,0:T(2,128)(2,1)}, u32[]{:S(2)}, u32[]{:S(2)}) collective-permute-start(bf16[34,1,2048]{2,1,0:T(2,128)(2,1)} %get-tuple-element.9), channel_id=1, source_target_pairs={{0,1},{1,2},{2,3},{3,4},{4,5},{5,6},{6,7},{8,9},{9,10},{10,11},{11... | collective-permute-start | bytes 417800 | tf_op jit(solution)/shard_map/ppermute | solution.py:22
  22.6 1.5 collective-permute-start.3
  24.0 0.0 copy-done.25
  24.1 0.0 copy-done.22
  24.1 1.3 convolution_bitcast_fusion.1
  25.4 0.2 reshape.69
  25.6 0.4 copy.32
  26.0 0.0 copy-done.11
  26.0 0.0 copy-start.12
  26.1 0.0 copy-start.15
  26.1 0.0 copy-start.16
  26.1 0.0 copy-start.17
  26.1 0.0 copy-start.18
  26.1 0.0 copy-start.19
  26.1 0.0 copy-start.20
  26.1 0.0 copy-start.21
  26.1 0.3 reshape.70.bias_ref
  26.4 0.0 copy-start.10
  26.4 0.0 collective-permute-done.2
  26.4 1.0 collective-permute-done.3
  27.5 6.3 %maximum_maximum_fusion = (bf16[34,33,2048]{2,1,0:T(8,128)(2,1)S(1)}, bf16[34,33,2048]{2,1,0:T(8,128)(2,1)S(1)}) fusion(bf16[1,32,2048]{2,1,0:T(8,128)(2,1)} %copy-done.11, bf16[32,32,2048]{2,1,0:T(8,128)(2,1)} %copy-done.9, bf16[1,32,2048]{2,1,0:T(8,128)(2,1)S(1)} %collective-permute-done, bf16[34,1,2048]{2,1,0:T(2,128)(2,1)} %collective-permute-done.2, ...), kind=kLoop, calls=%fused_computation.18 | loop fusion | flops 36765696 | bytes 13926400 | tf_op jit(solution)/shard_map/concatenate | solution.py:20
  33.7 0.0 copy-done.12
  33.7 0.0 copy-done.15
  33.7 0.0 copy-done.16
  33.8 0.0 copy-start.13
  33.8 15.2 %fusion.35 = (f32[2048]{0:T(1024)}, f32[32,32,2048]{2,1,0:T(8,128)}) fusion(f32[2048]{0:T(1024)S(1)} %bitcast.76, bf16[34,33,2048]{2,1,0:T(8,128)(2,1)S(1)} %get-tuple-element.8, f32[2048]{0:T(1024)S(1)} %bitcast.77, bf16[1,32,2048]{2,1,0:T(8,128)(2,1)S(1)} %copy-done.12, bf16[32,32,2048]{2,1,0:T(8,128)(2,1)S(1)} %copy-done.10, f32[2048]{0:T(1024)S(1)} %bitcast.70, ...), kind=kLoop, calls=%fused_computation.54 | loop fusion | flops 77592576 | bytes 38092800 | tf_op jit(solution)/shard_map/reduce_sum | solution.py:487
  49.0 6.3 %axis_sum_row.1.x_ref = f32[16,128]{1,0:T(8,128)} custom-call(f32[16,128]{1,0:T(8,128)} %bitcast.78), custom_call_target="tpu_custom_call" | custom-call | tf_op jit(solution)/shard_map/axis_sum_row/pallas_call | solution.py:210
  55.3 10.6 %axis_sum_col.1 = f32[16,128]{1,0:T(8,128)} custom-call(f32[16,128]{1,0:T(8,128)} %axis_sum_row.1.x_ref), custom_call_target="tpu_custom_call" | custom-call | tf_op jit(solution)/shard_map/axis_sum_col/pallas_call | solution.py:210
  65.9 0.7 broadcast_multiply_fusion
  66.7 0.0 copy-start.6
  66.7 0.3 convolution_bitcast_fusion.2
  67.0 1.5 fusion.29
  68.6 6.6 %fusion.19 = bf16[32,32,512]{2,1,0:T(8,128)(2,1)S(1)} fusion(bf16[32,32,512]{2,1,0:T(8,128)(2,1)} %param.24, bf16[2048,512]{1,0:T(8,128)(2,1)} %param.31, f32[32,32,2048]{2,1,0:T(8,128)} %get-tuple-element.6, f32[2048]{0:T(1024)S(1)} %add_divide_fusion), kind=kOutput, calls=%fused_computation.32 | convolution fusion | flops 2153250816 | bytes 12591104 | tf_op jit(solution)/shard_map/dot_general | solution.py:494
  75.2 0.0 copy-start.23
  75.2 0.0 copy-start.24
  75.2 0.0 copy-start.7
  75.2 0.0 copy-start.8
  75.2 23.3 %mixer_blocks.1 = bf16[1024,512]{1,0:T(8,128)(2,1)S(1)} custom-call(bf16[1024,512]{1,0:T(8,128)(2,1)S(1)} %bitcast.64, f32[1,512]{1,0:T(1,128)S(1)} %bitcast.60, f32[2,256,128]{2,1,0:T(8,128)S(1)} %reshape.70.bias_ref, f32[1,512]{1,0:T(1,128)S(1)} %bitcast.61, bf16[512,1536]{1,0:T(8,128)(2,1)S(1)} %copy-done.1, bf16[512,512]{1,0:T(8,128)(2,1)S(1)} %copy-done.3, ...), custom_call_target="tpu_custom_call" | custom-call | flops 6442450944 | bytes 12582912 | tf_op jit(solution)/shard_map/mixer_blocks/pallas_call | solution.py:367
  98.5 1.1 copy.26
  99.6 4.6 %all-to-all-start = ((bf16[32,32,512]{2,1,0:T(8,128)(2,1)}), bf16[32,32,512]{2,1,0:T(8,128)(2,1)S(1)}, u32[]{:S(2)}, u32[]{:S(2)}) async-start(bf16[32,32,512]{2,1,0:T(8,128)(2,1)} %bitcast.65), calls=%async_computation | async-start | bytes 2097152 | tf_op jit(solution)/shard_map/all_to_all | solution.py:428
  104.2 0.0 copy-done.23
  104.2 0.0 copy-done.24
  104.2 1.3 convolution_bitcast_fusion
  105.5 1.0 reshape.73
  106.5 2.2 %copy.31 = f32[2,2,4,64,64]{4,1,3,2,0:T(2,128)} copy(f32[2,2,4,64,64]{4,3,2,1,0:T(8,128)} %reshape.73) | data formatting | bytes 524288 | tf_op jit(solution)/shard_map/reshape | solution.py:400
  108.8 1.3 reshape.74.bias_ref
  110.1 21.3 %all-to-all-done = bf16[32,32,512]{2,1,0:T(8,128)(2,1)S(1)} async-done(((bf16[32,32,512]{2,1,0:T(8,128)(2,1)}), bf16[32,32,512]{2,1,0:T(8,128)(2,1)S(1)}, u32[]{:S(2)}, u32[]{:S(2)}) %all-to-all-start) | async-done | bytes 1048608 | tf_op jit(solution)/shard_map/all_to_all | solution.py:428
  131.4 1.4 copy-done.2
  132.8 1.0 copy-done.4
  133.9 23.6 %mixer_strided.1 = bf16[1024,512]{1,0:T(8,128)(2,1)S(1)} custom-call(bf16[1024,512]{1,0:T(8,128)(2,1)S(1)} %bitcast.57, f32[1,512]{1,0:T(1,128)S(1)} %bitcast.62, f32[2,256,128]{2,1,0:T(8,128)S(1)} %reshape.74.bias_ref, f32[1,512]{1,0:T(1,128)S(1)} %bitcast.63, bf16[512,1536]{1,0:T(8,128)(2,1)S(1)} %copy-done.2, bf16[512,512]{1,0:T(8,128)(2,1)S(1)} %copy-done.4, ...), custom_call_target="tpu_custom_call" | custom-call | flops 6442450944 | bytes 12582912 | tf_op jit(solution)/shard_map/mixer_strided/pallas_call | solution.py:367
  157.4 29.6 %all_to_all.10 = bf16[32,32,512]{2,1,0:T(8,128)(2,1)S(1)} all-to-all(bf16[32,32,512]{2,1,0:T(8,128)(2,1)S(1)} %bitcast.59), channel_id=1, replica_groups=mesh['row'=4,'col'=8] {'row','col'}, dimensions={0} | all-to-all | bytes 2097152 | tf_op jit(solution)/shard_map/all_to_all | solution.py:433
  187.0 1.1 copy.28
  (24 shorter events, 0.1 us)
Async XLA Ops:
  0.0 1.7 copy-start
  0.0 24.0 %copy-start.25 = (s32[4096]{0:T(1024)S(1)}, s32[4096]{0:T(1024)}, u32[]{:S(2)}) copy-start(s32[4096]{0:T(1024)} %constant.20.clone) | copy-start | bytes 49156
  0.0 13.1 %copy-start.14 = (f32[9,2048]{1,0:T(8,128)S(1)}, f32[9,2048]{1,0:T(8,128)}, u32[]{:S(2)}) copy-start(f32[9,2048]{1,0:T(8,128)} %param.28) | copy-start | bytes 221188
  0.0 24.1 %copy-start.22 = (f32[16,225]{1,0:T(8,128)S(1)}, f32[16,225]{1,0:T(8,128)}, u32[]{:S(2)}) copy-start(f32[16,225]{1,0:T(8,128)} %param.35) | copy-start | bytes 43204
  6.9 12.4 %copy-start.9 = (bf16[32,32,2048]{2,1,0:T(8,128)(2,1)}, bf16[32,32,2048]{2,1,0:T(8,128)(2,1)S(1)}, u32[]{:S(2)}) copy-start(bf16[32,32,2048]{2,1,0:T(8,128)(2,1)S(1)} %fusion.7) | copy-start | bytes 12582916
  6.9 7.6 %collective-permute-start = (bf16[1,32,2048]{2,1,0:T(8,128)(2,1)S(1)}, bf16[1,32,2048]{2,1,0:T(8,128)(2,1)S(1)}, u32[]{:S(2)}, u32[]{:S(2)}) collective-permute-start(bf16[1,32,2048]{2,1,0:T(8,128)(2,1)S(1)} %get-tuple-element.11), channel_id=1, source_target_pairs={{0,8},{8,16},{16,24},{1,9},{9,17},{17,25},{2,10},{10,18},{18,26},{... | collective-permute-start | bytes 393224 | tf_op jit(solution)/shard_map/ppermute | solution.py:22
  11.8 7.5 %collective-permute-start.1 = (bf16[1,32,2048]{2,1,0:T(8,128)(2,1)S(1)}, bf16[1,32,2048]{2,1,0:T(8,128)(2,1)S(1)}, u32[]{:S(2)}, u32[]{:S(2)}) collective-permute-start(bf16[1,32,2048]{2,1,0:T(8,128)(2,1)S(1)} %get-tuple-element.12), channel_id=1, source_target_pairs={{8,0},{16,8},{24,16},{9,1},{17,9},{25,17},{10,2},{18,10},{26,18},{... | collective-permute-start | bytes 393224 | tf_op jit(solution)/shard_map/ppermute | solution.py:24
  19.3 6.8 %copy-start.11 = (bf16[1,32,2048]{2,1,0:T(8,128)(2,1)}, bf16[1,32,2048]{2,1,0:T(8,128)(2,1)S(1)}, u32[]{:S(2)}) copy-start(bf16[1,32,2048]{2,1,0:T(8,128)(2,1)S(1)} %collective-permute-done.1) | copy-start | bytes 393220
  20.6 5.9 %collective-permute-start.2 = (bf16[34,1,2048]{2,1,0:T(2,128)(2,1)}, bf16[34,1,2048]{2,1,0:T(2,128)(2,1)}, u32[]{:S(2)}, u32[]{:S(2)}) collective-permute-start(bf16[34,1,2048]{2,1,0:T(2,128)(2,1)} %get-tuple-element.9), channel_id=1, source_target_pairs={{0,1},{1,2},{2,3},{3,4},{4,5},{5,6},{6,7},{8,9},{9,10},{10,11},{11... | collective-permute-start | bytes 417800 | tf_op jit(solution)/shard_map/ppermute | solution.py:22
  22.6 4.9 %collective-permute-start.3 = (bf16[34,1,2048]{2,1,0:T(2,128)(2,1)}, bf16[34,1,2048]{2,1,0:T(2,128)(2,1)}, u32[]{:S(2)}, u32[]{:S(2)}) collective-permute-start(bf16[34,1,2048]{2,1,0:T(2,128)(2,1)} %get-tuple-element.10), channel_id=1, source_target_pairs={{1,0},{2,1},{3,2},{4,3},{5,4},{6,5},{7,6},{9,8},{10,9},{11,10},{12... | collective-permute-start | bytes 417800 | tf_op jit(solution)/shard_map/ppermute | solution.py:24
  26.0 7.7 %copy-start.12 = (bf16[1,32,2048]{2,1,0:T(8,128)(2,1)S(1)}, bf16[1,32,2048]{2,1,0:T(8,128)(2,1)}, u32[]{:S(2)}) copy-start(bf16[1,32,2048]{2,1,0:T(8,128)(2,1)} %copy-done.11) | copy-start | bytes 393220
  26.1 7.7 %copy-start.15 = (f32[1,2048]{1,0:T(1,128)S(1)}, f32[1,2048]{1,0:T(1,128)}, u32[]{:S(2)}) copy-start(f32[1,2048]{1,0:T(1,128)} %get-tuple-element.15) | copy-start | bytes 24580
  26.1 7.7 %copy-start.16 = (f32[1,2048]{1,0:T(1,128)S(1)}, f32[1,2048]{1,0:T(1,128)}, u32[]{:S(2)}) copy-start(f32[1,2048]{1,0:T(1,128)} %get-tuple-element.16) | copy-start | bytes 24580
  26.1 7.7 %copy-start.17 = (f32[1,2048]{1,0:T(1,128)S(1)}, f32[1,2048]{1,0:T(1,128)}, u32[]{:S(2)}) copy-start(f32[1,2048]{1,0:T(1,128)} %get-tuple-element.17) | copy-start | bytes 24580
  26.1 7.7 %copy-start.18 = (f32[1,2048]{1,0:T(1,128)S(1)}, f32[1,2048]{1,0:T(1,128)}, u32[]{:S(2)}) copy-start(f32[1,2048]{1,0:T(1,128)} %get-tuple-element.18) | copy-start | bytes 24580
  26.1 7.7 %copy-start.19 = (f32[1,2048]{1,0:T(1,128)S(1)}, f32[1,2048]{1,0:T(1,128)}, u32[]{:S(2)}) copy-start(f32[1,2048]{1,0:T(1,128)} %get-tuple-element.19) | copy-start | bytes 24580
  26.1 7.7 %copy-start.20 = (f32[1,2048]{1,0:T(1,128)S(1)}, f32[1,2048]{1,0:T(1,128)}, u32[]{:S(2)}) copy-start(f32[1,2048]{1,0:T(1,128)} %get-tuple-element.20) | copy-start | bytes 24580
  26.1 7.7 %copy-start.21 = (f32[1,2048]{1,0:T(1,128)S(1)}, f32[1,2048]{1,0:T(1,128)}, u32[]{:S(2)}) copy-start(f32[1,2048]{1,0:T(1,128)} %get-tuple-element.21) | copy-start | bytes 24580
  26.4 7.4 %copy-start.10 = (bf16[32,32,2048]{2,1,0:T(8,128)(2,1)S(1)}, bf16[32,32,2048]{2,1,0:T(8,128)(2,1)}, u32[]{:S(2)}) copy-start(bf16[32,32,2048]{2,1,0:T(8,128)(2,1)} %copy-done.9) | copy-start | bytes 12582916
  33.8 32.8 %copy-start.13 = (bf16[2048,128]{1,0:T(8,128)(2,1)S(1)}, bf16[2048,128]{1,0:T(8,128)(2,1)}, u32[]{:S(2)}) copy-start(bf16[2048,128]{1,0:T(8,128)(2,1)} %param.29) | copy-start | bytes 1572868
  66.7 8.5 %copy-start.1 = (bf16[512,1536]{1,0:T(8,128)(2,1)S(1)}, bf16[512,1536]{1,0:T(8,128)(2,1)}, u32[]{:S(2)}) copy-start(bf16[512,1536]{1,0:T(8,128)(2,1)} %proj_hbm.2) | copy-start | bytes 4718596
  66.7 8.5 %copy-start.3 = (bf16[512,512]{1,0:T(8,128)(2,1)S(1)}, bf16[512,512]{1,0:T(8,128)(2,1)}, u32[]{:S(2)}) copy-start(bf16[512,512]{1,0:T(8,128)(2,1)} %out_hbm.2) | copy-start | bytes 1572868
  66.7 8.5 %copy-start.5 = (f32[512]{0:T(512)S(1)}, f32[512]{0:T(512)}, u32[]{:S(2)}) copy-start(f32[512]{0:T(512)} %param.32) | copy-start | bytes 6148
  66.7 8.5 %copy-start.6 = (f32[512]{0:T(512)S(1)}, f32[512]{0:T(512)}, u32[]{:S(2)}) copy-start(f32[512]{0:T(512)} %param.36) | copy-start | bytes 6148
  75.2 29.0 %copy-start.23 = (f32[16,225]{1,0:T(8,128)S(1)}, f32[16,225]{1,0:T(8,128)}, u32[]{:S(2)}) copy-start(f32[16,225]{1,0:T(8,128)} %param.42) | copy-start | bytes 43204
  75.2 29.0 %copy-start.24 = (s32[4096]{0:T(1024)S(1)}, s32[4096]{0:T(1024)}, u32[]{:S(2)}) copy-start(s32[4096]{0:T(1024)} %constant.21.clone) | copy-start | bytes 49156
  75.2 56.2 %copy-start.7 = (f32[512]{0:T(512)S(1)}, f32[512]{0:T(512)}, u32[]{:S(2)}) copy-start(f32[512]{0:T(512)} %param.39) | copy-start | bytes 6148
  75.2 56.2 %copy-start.8 = (f32[512]{0:T(512)S(1)}, f32[512]{0:T(512)}, u32[]{:S(2)}) copy-start(f32[512]{0:T(512)} %param.43) | copy-start | bytes 6148
  99.6 31.9 %all-to-all-start = ((bf16[32,32,512]{2,1,0:T(8,128)(2,1)}), bf16[32,32,512]{2,1,0:T(8,128)(2,1)S(1)}, u32[]{:S(2)}, u32[]{:S(2)}) async-start(bf16[32,32,512]{2,1,0:T(8,128)(2,1)} %bitcast.65), calls=%async_computation | async-start | bytes 2097152 | tf_op jit(solution)/shard_map/all_to_all | solution.py:428
  131.4 1.4 copy-start.2
  132.8 1.0 copy-start.4
where the time goes:
time: 189 us; the launch traced here: 188 us
  Pallas kernels  63.7 us (34%)
  blocking collectives  29.6 us (16%)
  waiting for transfers between devices  27.8 us (15%)
  other arithmetic  23.5 us (12%)
  matrix products  16.3 us (9%)
  starting transfers between devices  14.2 us (8%)
  local copies, waits for them, and re-layouts  12.5 us (7%)
    pallas_call x2, Pallas kernels, mixer(): pl.pallas_call(functools.partial(mixer_kernel, layout, feats // heads_cou...  46.8 us
    all_to_all x1, blocking collectives, grid_sublayers(): lax.all_to_all(out.reshape(devices, -1, feats), ('row', 'col'), split_axi...  29.6 us
    all_to_all x1, waiting for transfers between devices, grid_sublayers(): lax.all_to_all(sent, ('row', 'col'), split_axis=0, concat_axis=0, tiled=T...  21.3 us
    pallas_call x2, Pallas kernels, axis_sum(): pl.pallas_call(functools.partial(axis_sum_kernel, axis, count), out_shape...  16.9 us
    reduce_sum x1, other arithmetic, per_device(): local_sums = jnp.sum(depthwise, axis=(0, 1)).reshape(-1, 128)  15.2 us
    ppermute x2, starting transfers between devices, extended(): lax.ppermute(tail, axis, [(i, (i + 1) % count) for i in range(ends)])  6.9 us
    dot_general x1, matrix products, per_device(): jnp.dot(gated, project_weight, preferred_element_type=jnp.float32)  6.57 us
    concatenate x1, other arithmetic, extended(): jnp.concatenate([lax.ppermute(tail, axis, [(i, (i + 1) % count) for i in...  6.26 us
  transfers between devices with their start and end apart: 5, of which 4 were waited for; matrix products, arithmetic and copies ran while one was open for 5% of the time, Pallas kernels for 0%

commit v1 on v0

--- a/solution.py
+++ b/solution.py
@@ -363,7 +363,7 @@
     rows, feats = x.shape
     vmem = pl.BlockSpec(memory_space=pltpu.VMEM)
     hbm = pl.BlockSpec(memory_space=pl.ANY)
-    flops = 2 * rows * feats * (4 * feats + 2 * up.shape[1])
+    flops = 8 * rows * feats * (4 * feats + 2 * up.shape[1])
     return pl.pallas_call(
         functools.partial(mixer_kernel, layout, feats // heads_count),
         out_shape=jax.ShapeDtypeStruct((rows, feats), jnp.bfloat16),
@@ -403,41 +403,51 @@
     )
 
 
-def grid_sublayers(section, run, grid_table):
+def split_sublayers(conv_out, run_block, run_grid, block_table, grid_table):
     row_devices = lax.axis_size("row")
     col_devices = lax.axis_size("col")
-    row_count, col_count, feats = section.shape
+    row_count, col_count, feats = conv_out.shape
     plain = np.arange(WIN * WIN)
+    block_bias = key_major_bias(block_table, plain // WIN, plain % WIN)
     if row_devices > WIN or col_devices > WIN:
-        windows = grid_layout(section)
+        section = run_block(conv_out.reshape(-1, feats), ("blocks", col_count), block_bias)
+        windows = grid_layout(section.reshape(row_count, col_count, feats))
         count = windows.shape[0]
         bias = key_major_bias(grid_table, plain // WIN, plain % WIN)
-        out = run(windows.transpose(1, 0, 2).reshape(-1, feats), ("strided", count), bias)
+        out = run_grid(windows.transpose(1, 0, 2).reshape(-1, feats), ("strided", count), bias)
         out = out.reshape(WIN * WIN, count, feats).transpose(1, 0, 2)
         return spatial_layout(out, row_count, col_count)
     devices = row_devices * col_devices
     row_fold, col_fold = WIN // row_devices, WIN // col_devices
     row_rest, col_rest = row_count // row_fold, col_count // col_fold
-    count = row_rest * col_rest // devices
+    parts = row_rest // WIN
+    count = WIN * col_rest // devices
     pieces = col_rest // count
-    sent = (
-        section.reshape(row_fold, row_rest, col_fold, pieces, count, feats)
-        .transpose(1, 3, 0, 2, 4, 5)
-        .reshape(devices, row_fold * col_fold * count, feats)
-    )
-    got = lax.all_to_all(sent, ("row", "col"), split_axis=0, concat_axis=0, tiled=True)
     order = np.arange(WIN * WIN).reshape(row_devices, col_devices, row_fold, col_fold)
     at = np.indices(order.shape).reshape(4, -1)
-    bias = key_major_bias(grid_table, at[0] * row_fold + at[2], at[1] * col_fold + at[3])
-    out = run(got.reshape(-1, feats), ("strided", count), bias)
-    back = lax.all_to_all(
-        out.reshape(devices, -1, feats), ("row", "col"), split_axis=0, concat_axis=0, tiled=True
-    )
-    return (
-        back.reshape(row_rest, pieces, row_fold, col_fold, count, feats)
-        .transpose(2, 0, 3, 1, 4, 5)
-        .reshape(row_count, col_count, feats)
-    )
+    grid_bias = key_major_bias(grid_table, at[0] * row_fold + at[2], at[1] * col_fold + at[3])
+    strips = conv_out.reshape(row_fold, parts, WIN, col_count, feats)
+    results = []
+    for part in range(parts):
+        section = run_block(
+            strips[:, part].reshape(-1, feats), ("blocks", col_count), block_bias
+        )
+        sent = (
+            section.reshape(row_fold, WIN, col_fold, pieces, count, feats)
+            .transpose(1, 3, 0, 2, 4, 5)
+            .reshape(devices, row_fold * col_fold * count, feats)
+        )
+        got = lax.all_to_all(sent, ("row", "col"), split_axis=0, concat_axis=0, tiled=True)
+        out = run_grid(got.reshape(-1, feats), ("strided", count), grid_bias)
+        back = lax.all_to_all(
+            out.reshape(devices, -1, feats), ("row", "col"), split_axis=0, concat_axis=0, tiled=True
+        )
+        results.append(
+            back.reshape(WIN, pieces, row_fold, col_fold, count, feats)
+            .transpose(2, 0, 3, 1, 4, 5)
+            .reshape(row_fold, WIN, col_count, feats)
+        )
+    return jnp.stack(results, axis=1).reshape(row_count, col_count, feats)
 
 
 def per_device(
@@ -493,20 +503,20 @@
         latent.astype(jnp.float32)
         + jnp.dot(gated, project_weight, preferred_element_type=jnp.float32)
     ).astype(jnp.bfloat16)
-    plain = np.arange(WIN * WIN)
-    section = mixer(
-        conv_out.reshape(-1, channels), ("blocks", col_count), block_gain, block_projection,
-        block_output, key_major_bias(block_table, plain // WIN, plain % WIN), first_gain,
-        first_expand, first_reduce, block_table.shape[0],
-    ).reshape(row_count, col_count, channels)
-
-    def run(cells, layout, bias):
+
+    def run_block(cells, layout, bias):
+        return mixer(
+            cells, layout, block_gain, block_projection, block_output, bias, first_gain,
+            first_expand, first_reduce, block_table.shape[0],
+        )
+
+    def run_grid(cells, layout, bias):
         return mixer(
             cells, layout, grid_gain, grid_projection, grid_output, bias, second_gain,
             second_expand, second_reduce, grid_table.shape[0],
         )
 
-    return grid_sublayers(section, run, grid_table)
+    return split_sublayers(conv_out, run_block, run_grid, block_table, grid_table)
 
 
 def solution(mesh):

time: 189 us -> 184 us (0.974)
  blocking collectives: 29.6 us -> 0 us
  starting transfers between devices: 14.2 us -> 31.6 us
  local copies, waits for them, and re-layouts: 12.5 us -> 24.4 us
  waiting for transfers between devices: 27.8 us -> 18.6 us
  other arithmetic: 23.5 us -> 26.1 us
    all_to_all x1 -> x0, blocking collectives: 29.6 us -> none  [grid_sublayers(): lax.all_to_all(out.reshape(devices, -1, feats), ('row', 'col'), split_axi...]
    all_to_all x1 -> x4, starting transfers between devices: 4.59 us -> 22 us  [the longest x2 11.7 us: split_sublayers(): lax.all_to_all(out.reshape(devices, -1, feats), ('row', 'col'), split_axi...]
    unnamed x52 -> x70, local copies, waits for them, and re-layouts: 4.2 us -> 17.5 us
    all_to_all x1 -> x4, waiting for transfers between devices: 21.3 us -> 15.1 us  [the longest x2 15.1 us: split_sublayers(): lax.all_to_all(out.reshape(devices, -1, feats), ('row', 'col'), split_axi...]
    reshape x4, local copies, waits for them, and re-layouts: 3.88 us -> 1.24 us  [key_major_bias(): spread.reshape(head_count // 8, 2, 4, tokens, tokens)]
    ppermute x2, waiting for transfers between devices: 5.77 us -> 3.43 us  [extended(): lax.ppermute(head, axis, [((i + 1) % count, i) for i in range(ends)])]
    pallas_call x2 -> x4, Pallas kernels: 46.8 us -> 48.3 us  [mixer(): pl.pallas_call(functools.partial(mixer_kernel, layout, feats // heads_cou...]
  transfers between devices with their start and end apart: 5 -> 8, of which waited for: 4 -> 2; matrix products, arithmetic and copies ran while one was open for 5% -> 5% of each run, Pallas kernels for 0% -> 20%
where the time goes in v1:
time: 184 us; the launch traced here: 183 us
  Pallas kernels  64.7 us (35%)
  starting transfers between devices  31.6 us (17%)
  other arithmetic  26.1 us (14%)
  local copies, waits for them, and re-layouts  24.4 us (13%)
  waiting for transfers between devices  18.6 us (10%)
  matrix products  17 us (9%)
    pallas_call x4, Pallas kernels, mixer(): pl.pallas_call(functools.partial(mixer_kernel, layout, feats // heads_cou...  48.3 us
    unnamed x70, local copies, waits for them, and re-layouts  17.5 us
    pallas_call x2, Pallas kernels, axis_sum(): pl.pallas_call(functools.partial(axis_sum_kernel, axis, count), out_shape...  16.4 us
    reduce_sum x1, other arithmetic, per_device(): local_sums = jnp.sum(depthwise, axis=(0, 1)).reshape(-1, 128)  15.2 us
    all_to_all x2, waiting for transfers between devices, split_sublayers(): lax.all_to_all(out.reshape(devices, -1, feats), ('row', 'col'), split_axi...  15.1 us
    all_to_all x2, starting transfers between devices, split_sublayers(): lax.all_to_all(out.reshape(devices, -1, feats), ('row', 'col'), split_axi...  11.7 us
    all_to_all x2, starting transfers between devices, split_sublayers(): lax.all_to_all(sent, ('row', 'col'), split_axis=0, concat_axis=0, tiled=T...  10.3 us
    ppermute x2, starting transfers between devices, extended(): lax.ppermute(tail, axis, [(i, (i + 1) % count) for i in range(ends)])  6.85 us
  transfers between devices with their start and end apart: 8, of which 2 were waited for; matrix products, arithmetic and copies ran while one was open for 5% of the time, Pallas kernels for 20%

profile of v1, /device:TPU:0, one launch (start us, length us, event | category | flops | bytes accessed | tf_op | source)
XLA Modules:
  0.0 182.9 jit_solution(2346358766373277812)
XLA Ops:
  0.0 1.6 copy-done
  1.7 5.2 %fusion.7 = bf16[32,32,2048]{2,1,0:T(8,128)(2,1)S(1)} fusion(bf16[512,2048]{1,0:T(8,128)(2,1)S(1)} %copy-done, bf16[32,32,512]{2,1,0:T(8,128)(2,1)} %param.24, f32[512]{0:T(512)} %param.26, f32[512]{0:T(512)} %param.25), kind=kOutput, calls=%fused_computation.9 | convolution fusion | flops 2168455168 | bytes 7344128 | tf_op jit(solution)/shard_map/dot_general | solution.py:482
  6.9 1.9 %copy-done.20 = bf16[32,32,2048]{2,1,0:T(8,128)(2,1)} copy-done((bf16[32,32,2048]{2,1,0:T(8,128)(2,1)}, bf16[32,32,2048]{2,1,0:T(8,128)(2,1)S(1)}, u32[]{:S(2)}) %copy-start.20) | copy-done | bytes 4194328
  8.8 0.7 fusion.37
  9.5 4.9 %collective-permute-start = (bf16[1,32,2048]{2,1,0:T(8,128)(2,1)}, bf16[1,32,2048]{2,1,0:T(8,128)(2,1)S(1)}, u32[]{:S(2)}, u32[]{:S(2)}) collective-permute-start(bf16[1,32,2048]{2,1,0:T(8,128)(2,1)} %get-tuple-element.11), channel_id=1, source_target_pairs={{0,8},{8,16},{16,24},{1,9},{9,17},{17,25},{2,10},{10,18},{18,26},{... | collective-permute-start | bytes 393224 | tf_op jit(solution)/shard_map/ppermute | solution.py:22
  14.4 1.3 collective-permute-start.1
  15.7 0.7 fusion.39
  16.4 1.3 convolution_bitcast_fusion.1
  17.7 0.2 reshape.87
  17.9 0.4 copy.42
  18.3 0.3 reshape.88.bias_ref
  18.6 0.0 collective-permute-done
  18.6 3.4 %collective-permute-done.1 = bf16[1,32,2048]{2,1,0:T(8,128)(2,1)S(1)} collective-permute-done((bf16[1,32,2048]{2,1,0:T(8,128)(2,1)S(1)}, bf16[1,32,2048]{2,1,0:T(8,128)(2,1)S(1)}, u32[]{:S(2)}, u32[]{:S(2)}) %collective-permute-start.1) | collective-permute-done | bytes 131104 | tf_op jit(solution)/shard_map/ppermute | solution.py:24
  22.1 2.8 %pad_maximum_fusion.6 = (bf16[34,1,2048]{2,1,0:T(2,128)(2,1)}, bf16[34,1,2048]{2,1,0:T(2,128)(2,1)}) fusion(bf16[1,32,2048]{2,1,0:T(8,128)(2,1)S(1)} %collective-permute-done.1, bf16[32,32,2048]{2,1,0:T(8,128)(2,1)} %copy-done.20, bf16[1,32,2048]{2,1,0:T(8,128)(2,1)S(1)} %collective-permute-done), kind=kLoop, calls=%fused_computation.47 | loop fusion | flops 835584 | bytes 4734976 | tf_op jit(solution)/shard_map/slice | solution.py:19
  24.9 2.0 %collective-permute-start.2 = (bf16[34,1,2048]{2,1,0:T(2,128)(2,1)}, bf16[34,1,2048]{2,1,0:T(2,128)(2,1)}, u32[]{:S(2)}, u32[]{:S(2)}) collective-permute-start(bf16[34,1,2048]{2,1,0:T(2,128)(2,1)} %get-tuple-element.9), channel_id=1, source_target_pairs={{0,1},{1,2},{2,3},{3,4},{4,5},{5,6},{6,7},{8,9},{9,10},{10,11},{11... | collective-permute-start | bytes 417800 | tf_op jit(solution)/shard_map/ppermute | solution.py:22
  26.9 1.5 collective-permute-start.3
  28.4 2.1 %convolution_bitcast_fusion = f32[16,4096]{1,0:T(8,128)S(1)} fusion(f32[16,225]{1,0:T(8,128)} %param.42, s32[4096]{0:T(1024)} %constant.21.clone), kind=kOutput, calls=%fused_computation.20 | convolution fusion | flops 177868800 | bytes 292928 | tf_op jit(solution)/shard_map/dot_general | solution.py:398
  30.4 0.2 reshape.92
  30.7 0.4 copy.41
  31.1 1.0 reshape.93.bias_ref
  32.2 0.0 collective-permute-done.3
  32.2 6.2 %maximum_maximum_fusion = (bf16[34,33,2048]{2,1,0:T(8,128)(2,1)S(1)}, bf16[34,33,2048]{2,1,0:T(8,128)(2,1)S(1)}) fusion(bf16[1,32,2048]{2,1,0:T(8,128)(2,1)} %copy-done.22, bf16[32,32,2048]{2,1,0:T(8,128)(2,1)} %copy-done.20, bf16[1,32,2048]{2,1,0:T(8,128)(2,1)S(1)} %collective-permute-done, bf16[34,1,2048]{2,1,0:T(2,128)(2,1)} %collective-permute-done.2, ...), kind=kLoop, calls=%fused_computation.18 | loop fusion | flops 36765696 | bytes 13926400 | tf_op jit(solution)/shard_map/concatenate | solution.py:20
  38.5 0.0 copy-start.24
  38.5 15.2 %fusion.35 = (f32[2048]{0:T(1024)}, f32[32,32,2048]{2,1,0:T(8,128)}) fusion(f32[2048]{0:T(1024)S(1)} %bitcast.108, bf16[34,33,2048]{2,1,0:T(8,128)(2,1)S(1)} %get-tuple-element.8, f32[2048]{0:T(1024)S(1)} %bitcast.109, bf16[1,32,2048]{2,1,0:T(8,128)(2,1)S(1)} %copy-done.23, bf16[32,32,2048]{2,1,0:T(8,128)(2,1)S(1)} %copy-done.21, f32[2048]{0:T(1024)S(1)} %bitcast.102, ...), kind=kLoop, calls=%fused_computation.57 | loop fusion | flops 77592576 | bytes 38092800 | tf_op jit(solution)/shard_map/reduce_sum | solution.py:497
  53.7 6.1 %axis_sum_row.1.x_ref = f32[16,128]{1,0:T(8,128)} custom-call(f32[16,128]{1,0:T(8,128)} %bitcast.110), custom_call_target="tpu_custom_call" | custom-call | tf_op jit(solution)/shard_map/axis_sum_row/pallas_call | solution.py:210
  59.8 10.4 %axis_sum_col.1 = f32[16,128]{1,0:T(8,128)} custom-call(f32[16,128]{1,0:T(8,128)} %axis_sum_row.1.x_ref), custom_call_target="tpu_custom_call" | custom-call | tf_op jit(solution)/shard_map/axis_sum_col/pallas_call | solution.py:210
  70.2 0.7 broadcast_multiply_fusion
  70.9 0.3 convolution_bitcast_fusion.2
  71.2 1.4 fusion.29
  72.6 0.0 copy-start.4
  72.6 0.0 copy-start.8
  72.6 0.0 copy-start.12
  72.6 0.0 copy-start.16
  72.7 0.0 copy-start.17
  72.7 6.7 %fusion.19 = bf16[32,32,512]{2,1,0:T(8,128)(2,1)S(1)} fusion(bf16[32,32,512]{2,1,0:T(8,128)(2,1)} %param.24, bf16[2048,512]{1,0:T(8,128)(2,1)} %param.31, f32[32,32,2048]{2,1,0:T(8,128)} %get-tuple-element.6, f32[2048]{0:T(1024)S(1)} %add_divide_fusion), kind=kOutput, calls=%fused_computation.32 | convolution fusion | flops 2153250816 | bytes 12591104 | tf_op jit(solution)/shard_map/dot_general | solution.py:504
  79.4 0.1 fusion.38
  79.6 11.9 %mixer_blocks.3 = bf16[512,512]{1,0:T(8,128)(2,1)S(1)} custom-call(bf16[512,512]{1,0:T(8,128)(2,1)S(1)} %bitcast.84, f32[1,512]{1,0:T(1,128)S(1)} %bitcast.85, f32[2,256,128]{2,1,0:T(8,128)S(1)} %reshape.88.bias_ref, f32[1,512]{1,0:T(1,128)S(1)} %bitcast.87, bf16[512,1536]{1,0:T(8,128)(2,1)S(1)} %copy-done.8, bf16[512,512]{1,0:T(8,128)(2,1)S(1)} %copy-done.12, ...), custom_call_target="tpu_custom_call" | custom-call | flops 12884901888 | bytes 12582912 | tf_op jit(solution)/shard_map/mixer_blocks/pallas_call | solution.py:367
  91.4 0.9 copy.31
  92.3 4.7 %all-to-all-start.2 = ((bf16[32,16,512]{2,1,0:T(8,128)(2,1)}), bf16[32,16,512]{2,1,0:T(8,128)(2,1)S(1)}, u32[]{:S(2)}, u32[]{:S(2)}) async-start(bf16[32,16,512]{2,1,0:T(8,128)(2,1)} %bitcast.94), calls=%async_computation.2 | async-start | bytes 1048576 | tf_op jit(solution)/shard_map/all_to_all | solution.py:440
  97.0 0.0 copy-start.5
  97.0 1.6 copy-done.5
  98.6 1.4 copy-done.9
  100.0 1.0 copy-done.13
  101.0 11.9 %mixer_blocks.2 = bf16[512,512]{1,0:T(8,128)(2,1)S(1)} custom-call(bf16[512,512]{1,0:T(8,128)(2,1)S(1)} %bitcast.83, f32[1,512]{1,0:T(1,128)S(1)} %bitcast.86, f32[2,256,128]{2,1,0:T(8,128)S(1)} %reshape.88.bias_ref, f32[1,512]{1,0:T(1,128)S(1)} %bitcast.88, bf16[512,1536]{1,0:T(8,128)(2,1)S(1)} %copy-done.9, bf16[512,512]{1,0:T(8,128)(2,1)S(1)} %copy-done.13, ...), custom_call_target="tpu_custom_call" | custom-call | flops 12884901888 | bytes 12582912 | tf_op jit(solution)/shard_map/mixer_blocks/pallas_call | solution.py:367
  112.9 0.9 copy.27
  113.7 5.6 %all-to-all-start = ((bf16[32,16,512]{2,1,0:T(8,128)(2,1)}), bf16[32,16,512]{2,1,0:T(8,128)(2,1)S(1)}, u32[]{:S(2)}, u32[]{:S(2)}) async-start(bf16[32,16,512]{2,1,0:T(8,128)(2,1)} %bitcast.93), calls=%async_computation | async-start | bytes 1048576 | tf_op jit(solution)/shard_map/all_to_all | solution.py:440
  119.4 0.9 copy-done.2
  120.3 1.6 copy-done.6
  121.9 1.4 copy-done.10
  123.3 1.0 copy-done.14
  124.4 11.9 %mixer_strided.3 = bf16[512,512]{1,0:T(8,128)(2,1)S(1)} custom-call(bf16[512,512]{1,0:T(8,128)(2,1)S(1)} %bitcast.78, f32[1,512]{1,0:T(1,128)S(1)} %bitcast.89, f32[2,256,128]{2,1,0:T(8,128)S(1)} %copy-done.2, f32[1,512]{1,0:T(1,128)S(1)} %bitcast.91, bf16[512,1536]{1,0:T(8,128)(2,1)S(1)} %copy-done.10, bf16[512,512]{1,0:T(8,128)(2,1)S(1)} %copy-done.14, ...), custom_call_target="tpu_custom_call" | custom-call | flops 12884901888 | bytes 12582912 | tf_op jit(solution)/shard_map/mixer_strided/pallas_call | solution.py:367
  136.3 0.0 copy-start.1
  136.3 0.8 copy-done.1
  137.1 0.0 all-to-all-done
  137.1 6.0 %all-to-all-start.3 = ((bf16[32,16,512]{2,1,0:T(8,128)(2,1)}), bf16[32,16,512]{2,1,0:T(8,128)(2,1)}, u32[]{:S(2)}, u32[]{:S(2)}) async-start(bf16[32,16,512]{2,1,0:T(8,128)(2,1)} %bitcast.80), calls=%async_computation.3 | async-start | bytes 1048576 | tf_op jit(solution)/shard_map/all_to_all | solution.py:442
  143.0 0.0 copy-start.7
  143.1 1.6 copy-done.7
  144.6 1.4 copy-done.11
  146.0 1.0 copy-done.15
  147.1 12.7 %mixer_strided.2 = bf16[512,512]{1,0:T(8,128)(2,1)} custom-call(bf16[512,512]{1,0:T(8,128)(2,1)S(1)} %bitcast.79, f32[1,512]{1,0:T(1,128)S(1)} %bitcast.90, f32[2,256,128]{2,1,0:T(8,128)S(1)} %copy-done.3, f32[1,512]{1,0:T(1,128)S(1)} %bitcast.92, bf16[512,1536]{1,0:T(8,128)(2,1)S(1)} %copy-done.11, bf16[512,512]{1,0:T(8,128)(2,1)S(1)} %copy-done.15, ...), custom_call_target="tpu_custom_call" | custom-call | flops 12884901888 | bytes 12582912 | tf_op jit(solution)/shard_map/mixer_strided/pallas_call | solution.py:367
  159.8 5.8 %all-to-all-start.1 = ((bf16[32,16,512]{2,1,0:T(8,128)(2,1)}), bf16[32,16,512]{2,1,0:T(8,128)(2,1)S(1)}, u32[]{:S(2)}, u32[]{:S(2)}) async-start(bf16[32,16,512]{2,1,0:T(8,128)(2,1)} %bitcast.31), calls=%async_computation.1 | async-start | bytes 1048576 | tf_op jit(solution)/shard_map/all_to_all | solution.py:442
  165.6 1.1 copy.39
  166.7 15.1 %all-to-all-done.1 = bf16[32,16,512]{2,1,0:T(8,128)(2,1)S(1)} async-done(((bf16[32,16,512]{2,1,0:T(8,128)(2,1)}), bf16[32,16,512]{2,1,0:T(8,128)(2,1)S(1)}, u32[]{:S(2)}, u32[]{:S(2)}) %all-to-all-start.1) | async-done | bytes 524320 | tf_op jit(solution)/shard_map/all_to_all | solution.py:442
  181.9 1.1 pad_maximum_fusion.3
  (53 shorter events, 0.2 us)
Async XLA Ops:
  0.0 1.7 copy-start
  0.0 16.3 %copy-start.34 = (s32[4096]{0:T(1024)S(1)}, s32[4096]{0:T(1024)}, u32[]{:S(2)}) copy-start(s32[4096]{0:T(1024)} %constant.20.clone) | copy-start | bytes 49156
  0.0 15.7 %copy-start.25 = (f32[9,2048]{1,0:T(8,128)S(1)}, f32[9,2048]{1,0:T(8,128)}, u32[]{:S(2)}) copy-start(f32[9,2048]{1,0:T(8,128)} %param.28) | copy-start | bytes 221188
  0.0 16.3 %copy-start.33 = (f32[16,225]{1,0:T(8,128)S(1)}, f32[16,225]{1,0:T(8,128)}, u32[]{:S(2)}) copy-start(f32[16,225]{1,0:T(8,128)} %param.35) | copy-start | bytes 43204
  6.9 2.0 %copy-start.20 = (bf16[32,32,2048]{2,1,0:T(8,128)(2,1)}, bf16[32,32,2048]{2,1,0:T(8,128)(2,1)S(1)}, u32[]{:S(2)}) copy-start(bf16[32,32,2048]{2,1,0:T(8,128)(2,1)S(1)} %fusion.7) | copy-start | bytes 12582916
  9.5 9.1 %collective-permute-start = (bf16[1,32,2048]{2,1,0:T(8,128)(2,1)}, bf16[1,32,2048]{2,1,0:T(8,128)(2,1)S(1)}, u32[]{:S(2)}, u32[]{:S(2)}) collective-permute-start(bf16[1,32,2048]{2,1,0:T(8,128)(2,1)} %get-tuple-element.11), channel_id=1, source_target_pairs={{0,8},{8,16},{16,24},{1,9},{9,17},{17,25},{2,10},{10,18},{18,26},{... | collective-permute-start | bytes 393224 | tf_op jit(solution)/shard_map/ppermute | solution.py:22
  14.4 7.7 %collective-permute-start.1 = (bf16[1,32,2048]{2,1,0:T(8,128)(2,1)S(1)}, bf16[1,32,2048]{2,1,0:T(8,128)(2,1)S(1)}, u32[]{:S(2)}, u32[]{:S(2)}) collective-permute-start(bf16[1,32,2048]{2,1,0:T(8,128)(2,1)S(1)} %get-tuple-element.12), channel_id=1, source_target_pairs={{8,0},{16,8},{24,16},{9,1},{17,9},{25,17},{10,2},{18,10},{26,18},{... | collective-permute-start | bytes 393224 | tf_op jit(solution)/shard_map/ppermute | solution.py:24
  22.1 8.4 %copy-start.22 = (bf16[1,32,2048]{2,1,0:T(8,128)(2,1)}, bf16[1,32,2048]{2,1,0:T(8,128)(2,1)S(1)}, u32[]{:S(2)}) copy-start(bf16[1,32,2048]{2,1,0:T(8,128)(2,1)S(1)} %collective-permute-done.1) | copy-start | bytes 393220
  24.9 7.3 %collective-permute-start.2 = (bf16[34,1,2048]{2,1,0:T(2,128)(2,1)}, bf16[34,1,2048]{2,1,0:T(2,128)(2,1)}, u32[]{:S(2)}, u32[]{:S(2)}) collective-permute-start(bf16[34,1,2048]{2,1,0:T(2,128)(2,1)} %get-tuple-element.9), channel_id=1, source_target_pairs={{0,1},{1,2},{2,3},{3,4},{4,5},{5,6},{6,7},{8,9},{9,10},{10,11},{11... | collective-permute-start | bytes 417800 | tf_op jit(solution)/shard_map/ppermute | solution.py:22
  26.9 5.3 %collective-permute-start.3 = (bf16[34,1,2048]{2,1,0:T(2,128)(2,1)}, bf16[34,1,2048]{2,1,0:T(2,128)(2,1)}, u32[]{:S(2)}, u32[]{:S(2)}) collective-permute-start(bf16[34,1,2048]{2,1,0:T(2,128)(2,1)} %get-tuple-element.10), channel_id=1, source_target_pairs={{1,0},{2,1},{3,2},{4,3},{5,4},{6,5},{7,6},{9,8},{10,9},{11,10},{12... | collective-permute-start | bytes 417800 | tf_op jit(solution)/shard_map/ppermute | solution.py:24
  31.1 7.4 %copy-start.23 = (bf16[1,32,2048]{2,1,0:T(8,128)(2,1)S(1)}, bf16[1,32,2048]{2,1,0:T(8,128)(2,1)}, u32[]{:S(2)}) copy-start(bf16[1,32,2048]{2,1,0:T(8,128)(2,1)} %copy-done.22) | copy-start | bytes 393220
  32.1 6.3 %copy-start.21 = (bf16[32,32,2048]{2,1,0:T(8,128)(2,1)S(1)}, bf16[32,32,2048]{2,1,0:T(8,128)(2,1)}, u32[]{:S(2)}) copy-start(bf16[32,32,2048]{2,1,0:T(8,128)(2,1)} %copy-done.20) | copy-start | bytes 12582916
  32.1 6.3 %copy-start.26 = (f32[1,2048]{1,0:T(1,128)S(1)}, f32[1,2048]{1,0:T(1,128)}, u32[]{:S(2)}) copy-start(f32[1,2048]{1,0:T(1,128)} %get-tuple-element.17) | copy-start | bytes 24580
  32.1 6.3 %copy-start.27 = (f32[1,2048]{1,0:T(1,128)S(1)}, f32[1,2048]{1,0:T(1,128)}, u32[]{:S(2)}) copy-start(f32[1,2048]{1,0:T(1,128)} %get-tuple-element.18) | copy-start | bytes 24580
  32.1 6.3 %copy-start.28 = (f32[1,2048]{1,0:T(1,128)S(1)}, f32[1,2048]{1,0:T(1,128)}, u32[]{:S(2)}) copy-start(f32[1,2048]{1,0:T(1,128)} %get-tuple-element.19) | copy-start | bytes 24580
  32.1 6.4 %copy-start.29 = (f32[1,2048]{1,0:T(1,128)S(1)}, f32[1,2048]{1,0:T(1,128)}, u32[]{:S(2)}) copy-start(f32[1,2048]{1,0:T(1,128)} %get-tuple-element.20) | copy-start | bytes 24580
  32.1 6.4 %copy-start.30 = (f32[1,2048]{1,0:T(1,128)S(1)}, f32[1,2048]{1,0:T(1,128)}, u32[]{:S(2)}) copy-start(f32[1,2048]{1,0:T(1,128)} %get-tuple-element.21) | copy-start | bytes 24580
  32.2 6.4 %copy-start.31 = (f32[1,2048]{1,0:T(1,128)S(1)}, f32[1,2048]{1,0:T(1,128)}, u32[]{:S(2)}) copy-start(f32[1,2048]{1,0:T(1,128)} %get-tuple-element.22) | copy-start | bytes 24580
  32.2 6.4 %copy-start.32 = (f32[1,2048]{1,0:T(1,128)S(1)}, f32[1,2048]{1,0:T(1,128)}, u32[]{:S(2)}) copy-start(f32[1,2048]{1,0:T(1,128)} %get-tuple-element.23) | copy-start | bytes 24580
  38.5 32.4 %copy-start.24 = (bf16[2048,128]{1,0:T(8,128)(2,1)S(1)}, bf16[2048,128]{1,0:T(8,128)(2,1)}, u32[]{:S(2)}) copy-start(bf16[2048,128]{1,0:T(8,128)(2,1)} %param.29) | copy-start | bytes 1572868
  72.6 6.9 %copy-start.4 = (bf16[512,2048]{1,0:T(8,128)(2,1)S(1)}, bf16[512,2048]{1,0:T(8,128)(2,1)}, u32[]{:S(2)}) copy-start(bf16[512,2048]{1,0:T(8,128)(2,1)} %up_hbm.6) | copy-start | bytes 6291460
  72.6 6.9 %copy-start.8 = (bf16[512,1536]{1,0:T(8,128)(2,1)S(1)}, bf16[512,1536]{1,0:T(8,128)(2,1)}, u32[]{:S(2)}) copy-start(bf16[512,1536]{1,0:T(8,128)(2,1)} %proj_hbm.6) | copy-start | bytes 4718596
  72.6 6.9 %copy-start.12 = (bf16[512,512]{1,0:T(8,128)(2,1)S(1)}, bf16[512,512]{1,0:T(8,128)(2,1)}, u32[]{:S(2)}) copy-start(bf16[512,512]{1,0:T(8,128)(2,1)} %out_hbm.6) | copy-start | bytes 1572868
  72.6 6.9 %copy-start.16 = (f32[512]{0:T(512)S(1)}, f32[512]{0:T(512)}, u32[]{:S(2)}) copy-start(f32[512]{0:T(512)} %param.32) | copy-start | bytes 6148
  72.7 6.9 %copy-start.17 = (f32[512]{0:T(512)S(1)}, f32[512]{0:T(512)}, u32[]{:S(2)}) copy-start(f32[512]{0:T(512)} %param.36) | copy-start | bytes 6148
  92.3 21.4 %all-to-all-start.2 = ((bf16[32,16,512]{2,1,0:T(8,128)(2,1)}), bf16[32,16,512]{2,1,0:T(8,128)(2,1)S(1)}, u32[]{:S(2)}, u32[]{:S(2)}) async-start(bf16[32,16,512]{2,1,0:T(8,128)(2,1)} %bitcast.94), calls=%async_computation.2 | async-start | bytes 1048576 | tf_op jit(solution)/shard_map/all_to_all | solution.py:440
  97.0 1.6 copy-start.5
  98.6 1.4 copy-start.9
  100.0 1.0 copy-start.13
  101.0 18.4 %copy-start.18 = (f32[512]{0:T(512)S(1)}, f32[512]{0:T(512)}, u32[]{:S(2)}) copy-start(f32[512]{0:T(512)} %param.39) | copy-start | bytes 6148
  101.0 18.4 %copy-start.19 = (f32[512]{0:T(512)S(1)}, f32[512]{0:T(512)}, u32[]{:S(2)}) copy-start(f32[512]{0:T(512)} %param.43) | copy-start | bytes 6148
  113.7 23.3 %all-to-all-start = ((bf16[32,16,512]{2,1,0:T(8,128)(2,1)}), bf16[32,16,512]{2,1,0:T(8,128)(2,1)S(1)}, u32[]{:S(2)}, u32[]{:S(2)}) async-start(bf16[32,16,512]{2,1,0:T(8,128)(2,1)} %bitcast.93), calls=%async_computation | async-start | bytes 1048576 | tf_op jit(solution)/shard_map/all_to_all | solution.py:440
  119.4 1.0 copy-start.2
  120.3 1.6 copy-start.6
  121.9 1.4 copy-start.10
  123.3 1.0 copy-start.14
  124.4 18.6 %copy-start.3 = (f32[2,256,128]{2,1,0:T(8,128)S(1)}, f32[2,256,128]{2,1,0:T(8,128)}, u32[]{:S(2)}) copy-start(f32[2,256,128]{2,1,0:T(8,128)} %reshape.93.bias_ref) | copy-start | bytes 786436
  136.3 0.8 copy-start.1
  137.1 22.7 %all-to-all-start.3 = ((bf16[32,16,512]{2,1,0:T(8,128)(2,1)}), bf16[32,16,512]{2,1,0:T(8,128)(2,1)}, u32[]{:S(2)}, u32[]{:S(2)}) async-start(bf16[32,16,512]{2,1,0:T(8,128)(2,1)} %bitcast.80), calls=%async_computation.3 | async-start | bytes 1048576 | tf_op jit(solution)/shard_map/all_to_all | solution.py:442
  143.0 1.6 copy-start.7
  144.6 1.4 copy-start.11
  146.0 1.0 copy-start.15
  159.8 22.0 %all-to-all-start.1 = ((bf16[32,16,512]{2,1,0:T(8,128)(2,1)}), bf16[32,16,512]{2,1,0:T(8,128)(2,1)S(1)}, u32[]{:S(2)}, u32[]{:S(2)}) async-start(bf16[32,16,512]{2,1,0:T(8,128)(2,1)} %bitcast.31), calls=%async_computation.1 | async-start | bytes 1048576 | tf_op jit(solution)/shard_map/all_to_all | solution.py:442

commit v2 on v1

--- a/solution.py
+++ b/solution.py
@@ -362,7 +362,7 @@
 def mixer(x, layout, gain, in_weight, out_weight, bias, late_gain, up, down, heads_count):
     rows, feats = x.shape
     vmem = pl.BlockSpec(memory_space=pltpu.VMEM)
-    hbm = pl.BlockSpec(memory_space=pl.ANY)
+    hbm = pl.BlockSpec(memory_space=pltpu.HBM)
     flops = 8 * rows * feats * (4 * feats + 2 * up.shape[1])
     return pl.pallas_call(
         functools.partial(mixer_kernel, layout, feats // heads_count),
@@ -378,7 +378,7 @@
             pltpu.VMEM(down.shape, jnp.bfloat16),
             pltpu.SemaphoreType.DMA((4,)),
         ],
-        compiler_params=pltpu.CompilerParams(vmem_limit_bytes=48 * 1024 * 1024),
+        compiler_params=pltpu.CompilerParams(vmem_limit_bytes=60 * 1024 * 1024),
         cost_estimate=pl.CostEstimate(
             flops=flops, bytes_accessed=12 * 1024 * 1024, transcendentals=0
         ),
@@ -450,6 +450,102 @@
     return jnp.stack(results, axis=1).reshape(row_count, col_count, feats)
 
 
+PAD = 8
+
+
+def conv_kernel(
+    row_count, col_count, flags, ext_ref, scale_ref, shift_ref, expand_ref, taps_ref,
+    o_ref, sums_ref, conv_in, expanded,
+):
+    wide = col_count + PAD
+    tall = row_count + 2
+    width = expand_ref.shape[1]
+    block = expanded.shape[-1]
+    bounds = [8 * k for k in range(row_count // 8)] + [tall]
+    for low, high in zip(bounds[:-1], bounds[1:]):
+        rows = slice(low * wide, high * wide)
+        conv_in[rows, :] = (
+            ext_ref[rows, :].astype(jnp.float32) * scale_ref[...] + shift_ref[...]
+        ).astype(jnp.bfloat16)
+    spot = lax.broadcasted_iota(jnp.int32, (1, PAD, block), 1)
+    side = jnp.where(spot == 0, flags[3], jnp.where(spot == PAD - 1, flags[2], 0.0))
+
+    def channels(step, carry):
+        lanes = pl.ds(pl.multiple_of(step * block, block), block)
+        for low, high in zip(bounds[:-1], bounds[1:]):
+            product = jnp.dot(
+                conv_in[low * wide : high * wide, :], expand_ref[:, lanes],
+                preferred_element_type=jnp.float32,
+            )
+            value = jax.nn.gelu(product, approximate=True).astype(jnp.bfloat16)
+            expanded[low:high] = value.astype(jnp.float32).reshape(high - low, wide, block)
+        expanded[0] = expanded[0] * flags[0]
+        expanded[tall - 1] = expanded[tall - 1] * flags[1]
+        expanded[:, col_count:, :] = expanded[:, col_count:, :] * side
+        for half in range(block // LANES):
+            inner = slice(half * LANES, (half + 1) * LANES)
+            outer = pl.ds(pl.multiple_of(step * block + half * LANES, LANES), LANES)
+            taps = [taps_ref[k : k + 1, outer] for k in range(9)]
+
+            def rows_of(group, total):
+                base = group * 4
+                held = [expanded[base + k, :, inner] for k in range(6)]
+                for k in range(4):
+                    parts = [
+                        held[k] * taps[side_step]
+                        + held[k + 1] * taps[3 + side_step]
+                        + held[k + 2] * taps[6 + side_step]
+                        for side_step in range(3)
+                    ]
+                    summed = (
+                        pltpu.roll(parts[0], 1, 0) + parts[1] + pltpu.roll(parts[2], wide - 1, 0)
+                    )[:col_count]
+                    deep = jax.nn.gelu(summed, approximate=True)
+                    total = total + jnp.sum(deep.reshape(col_count // 8, 8, LANES), axis=0)
+                    at = pl.ds(pl.multiple_of((base + k) * col_count, col_count), col_count)
+                    o_ref[at, outer] = deep.astype(o_ref.dtype)
+                return total
+
+            total = lax.fori_loop(0, row_count // 4, rows_of, jnp.zeros((8, LANES), jnp.float32))
+            sums_ref[:, outer] = jnp.sum(total, axis=0, keepdims=True)
+        return carry
+
+    lax.fori_loop(0, width // block, channels, 0)
+
+
+def depthwise_stage(latent, conv_scale, conv_shift, expand_weight, depth_kernel):
+    row_count, col_count, feats = latent.shape
+    width = expand_weight.shape[1]
+    row_at, col_at = lax.axis_index("row"), lax.axis_index("col")
+    flags = jnp.stack(
+        [row_at > 0, row_at < lax.axis_size("row") - 1, col_at > 0, col_at < lax.axis_size("col") - 1]
+    ).astype(jnp.float32)
+    tall = extended(latent, (("row", 0),), 1)
+    count = lax.axis_size("col")
+    ahead = [(i, i + 1) for i in range(count - 1)]
+    left = lax.ppermute(tall[:, col_count - 1 :], "col", ahead)
+    right = lax.ppermute(tall[:, :1], "col", [(b, a) for a, b in ahead])
+    blank = jnp.zeros((row_count + 2, PAD - 2, feats), latent.dtype)
+    ext = jnp.concatenate([tall, right, blank, left], axis=1).reshape(-1, feats)
+    vmem = pl.BlockSpec(memory_space=pltpu.VMEM)
+    block = 256
+    return pl.pallas_call(
+        functools.partial(conv_kernel, row_count, col_count),
+        out_shape=(
+            jax.ShapeDtypeStruct((row_count * col_count, width), jnp.bfloat16),
+            jax.ShapeDtypeStruct((1, width), jnp.float32),
+        ),
+        in_specs=[pl.BlockSpec(memory_space=pltpu.SMEM)] + [vmem] * 5,
+        out_specs=(vmem, vmem),
+        scratch_shapes=[
+            pltpu.VMEM(ext.shape, jnp.bfloat16),
+            pltpu.VMEM((row_count + 2, col_count + PAD, block), jnp.float32),
+        ],
+        compiler_params=pltpu.CompilerParams(vmem_limit_bytes=40 * 1024 * 1024),
+        name="conv_stage",
+    )(flags, ext, conv_scale[None], conv_shift[None], expand_weight, depth_kernel)
+
+
 def per_device(
     latent,
     conv_scale,
@@ -477,32 +573,18 @@
     row_devices = lax.axis_size("row")
     col_devices = lax.axis_size("col")
     row_count, col_count, channels = latent.shape
-    conv_in = (latent.astype(jnp.float32) * conv_scale + conv_shift).astype(jnp.bfloat16)
-    expanded = jax.nn.gelu(
-        jnp.dot(conv_in, expand_weight, preferred_element_type=jnp.float32), approximate=True
-    ).astype(jnp.bfloat16)
-    padded = extended(expanded, (("row", 0), ("col", 1)), 1)
-    summed = jnp.zeros((row_count, col_count, padded.shape[-1]), jnp.float32)
-    for offset in range(9):
-        down_step = offset // 3
-        side_step = offset % 3
-        summed = (
-            summed
-            + padded[down_step : down_step + row_count, side_step : side_step + col_count].astype(
-                jnp.float32
-            )
-            * depth_kernel[offset]
-        )
-    depthwise = jax.nn.gelu(summed, approximate=True)
-    local_sums = jnp.sum(depthwise, axis=(0, 1)).reshape(-1, 128)
+    depthwise, local_sums = depthwise_stage(
+        latent, conv_scale, conv_shift, expand_weight, depth_kernel
+    )
+    local_sums = local_sums.reshape(-1, LANES)
     channel_sums = axis_sum(axis_sum(local_sums, "row", 1), "col", 2).reshape(-1)
     pooled = channel_sums / (row_count * row_devices * col_count * col_devices)
     excite = squeeze_gate(pooled, squeeze_down, squeeze_up)
-    gated = (depthwise * excite).astype(jnp.bfloat16)
+    gated = (depthwise.astype(jnp.float32) * excite).astype(jnp.bfloat16)
     conv_out = (
-        latent.astype(jnp.float32)
+        latent.reshape(-1, channels).astype(jnp.float32)
         + jnp.dot(gated, project_weight, preferred_element_type=jnp.float32)
-    ).astype(jnp.bfloat16)
+    ).astype(jnp.bfloat16).reshape(row_count, col_count, channels)
 
     def run_block(cells, layout, bias):
         return mixer(

time: 184 us -> 176 us (0.957)
  Pallas kernels: 64.7 us -> 94.2 us
  other arithmetic: 26.1 us -> 4.93 us
  local copies, waits for them, and re-layouts: 24.4 us -> 14.6 us
  matrix products: 17 us -> 12.1 us
    pallas_call x0 -> x1, Pallas kernels: none -> 18.9 us  [depthwise_stage(): pl.pallas_call(functools.partial(conv_kernel, row_count, col_count), out_...]
    reduce_sum x1 -> x0, other arithmetic: 15.2 us -> none  [per_device(): local_sums = jnp.sum(depthwise, axis=(0, 1)).reshape(-1, 128)]
    unnamed x70 -> x26, local copies, waits for them, and re-layouts: 17.5 us -> 2.69 us
    pallas_call x4, Pallas kernels: 48.3 us -> 59.7 us  [mixer(): pl.pallas_call(functools.partial(mixer_kernel, layout, feats // heads_cou...]
    dot_general x1 -> x0, matrix products: 5.2 us -> none  [per_device(): jnp.dot(conv_in, expand_weight, preferred_element_type=jnp.float32)]
    ppermute x0 -> x2, starting transfers between devices: none -> 4.49 us  [the longest x1 3.21 us: depthwise_stage(): left = lax.ppermute(tall[:, col_count - 1:], 'col', ahead)]
    concatenate x1, other arithmetic: 6.23 us -> 2.02 us  [depthwise_stage(): ext = jnp.concatenate([tall, right, blank, left], axis=1).reshape(-1, feats)]
    ppermute x2 -> x1, waiting for transfers between devices: 3.43 us -> 0.01 us  [extended(): lax.ppermute(head, axis, [((i + 1) % count, i) for i in range(ends)])]
  transfers between devices with their start and end apart: 8 -> 8, of which waited for: 2 -> 3; matrix products, arithmetic and copies ran while one was open for 5% -> 7% of each run, Pallas kernels for 20% -> 26%
where the time goes in v2:
time: 176 us; the launch traced here: 175 us
  Pallas kernels  94.2 us (54%)
  starting transfers between devices  30.3 us (17%)
  waiting for transfers between devices  18 us (10%)
  local copies, waits for them, and re-layouts  14.6 us (8%)
  matrix products  12.1 us (7%)
  other arithmetic  4.93 us (3%)
    pallas_call x4, Pallas kernels, mixer(): pl.pallas_call(functools.partial(mixer_kernel, layout, feats // heads_cou...  59.7 us
    pallas_call x1, Pallas kernels, depthwise_stage(): pl.pallas_call(functools.partial(conv_kernel, row_count, col_count), out_...  18.9 us
    all_to_all x2, waiting for transfers between devices, split_sublayers(): lax.all_to_all(out.reshape(devices, -1, feats), ('row', 'col'), split_axi...  16.7 us
    pallas_call x2, Pallas kernels, axis_sum(): pl.pallas_call(functools.partial(axis_sum_kernel, axis, count), out_shape...  15.7 us
    all_to_all x2, starting transfers between devices, split_sublayers(): lax.all_to_all(sent, ('row', 'col'), split_axis=0, concat_axis=0, tiled=T...  10.4 us
    all_to_all x2, starting transfers between devices, split_sublayers(): lax.all_to_all(out.reshape(devices, -1, feats), ('row', 'col'), split_axi...  9.13 us
    ppermute x1, starting transfers between devices, extended(): lax.ppermute(tail, axis, [(i, (i + 1) % count) for i in range(ends)])  4.99 us
    dot_general x2, matrix products, key_major_bias(): spread = jnp.dot(table, chosen, precision=lax.Precision.HIGHEST)  4.84 us
  transfers between devices with their start and end apart: 8, of which 3 were waited for; matrix products, arithmetic and copies ran while one was open for 7% of the time, Pallas kernels for 26%

profile of v2, /device:TPU:0, one launch (start us, length us, event | category | flops | bytes accessed | tf_op | source)
XLA Modules:
  0.0 174.5 jit_solution(11350465313692883118)
XLA Ops:
  0.0 0.0 copy-start
  0.0 0.9 fusion.13
  0.9 5.0 %collective-permute-start = (bf16[1,32,512]{2,1,0:T(8,128)(2,1)S(1)}, bf16[1,32,512]{2,1,0:T(8,128)(2,1)S(1)}, u32[]{:S(2)}, u32[]{:S(2)}) collective-permute-start(bf16[1,32,512]{2,1,0:T(8,128)(2,1)S(1)} %get-tuple-element.14), channel_id=1, source_target_pairs={{0,8},{8,16},{16,24},{1,9},{9,17},{17,25},{2,10},{10,18},{18,26},{... | collective-permute-start | bytes 98312 | tf_op jit(solution)/shard_map/ppermute | solution.py:22
  5.9 1.3 collective-permute-start.1
  7.2 2.8 %convolution_bitcast_fusion.1 = f32[16,4096]{1,0:T(8,128)} fusion(f32[16,225]{1,0:T(8,128)} %param.35, s32[4096]{0:T(1024)} %constant.27.clone), kind=kOutput, calls=%fused_computation.2 | convolution fusion | flops 177868800 | bytes 292928 | tf_op jit(solution)/shard_map/dot_general | solution.py:398
  10.0 2.1 %convolution_bitcast_fusion = f32[16,4096]{1,0:T(8,128)S(1)} fusion(f32[16,225]{1,0:T(8,128)} %param.42, s32[4096]{0:T(1024)} %constant.28.clone), kind=kOutput, calls=%fused_computation.1 | convolution fusion | flops 177868800 | bytes 292928 | tf_op jit(solution)/shard_map/dot_general | solution.py:398
  12.1 0.0 collective-permute-done
  12.1 0.0 copy-done.8
  12.1 0.1 constant_dynamic-update-slice_fusion.1
  12.2 0.0 collective-permute-done.1
  12.2 0.0 copy-start.7
  12.2 0.9 fusion.11
  13.1 1.3 collective-permute-start.2
  14.4 3.2 %collective-permute-start.3 = (bf16[34,1,512]{2,1,0:T(2,128)(2,1)}, bf16[34,1,512]{2,1,0:T(2,128)(2,1)S(1)}, u32[]{:S(2)}, u32[]{:S(2)}) collective-permute-start(bf16[34,1,512]{2,1,0:T(2,128)(2,1)} %get-tuple-element.10), channel_id=1, source_target_pairs={{0,1},{1,2},{2,3},{3,4},{4,5},{5,6},{6,7},{8,9},{9,10},{10,11},{11... | collective-permute-start | bytes 104456 | tf_op jit(solution)/shard_map/ppermute | solution.py:526
  17.6 0.0 copy-done.7
  17.7 0.1 add_convert_fusion.flags
  17.7 1.1 reshape.78
  18.9 0.4 copy.42
  19.3 1.0 reshape.79.bias_ref
  20.3 0.2 reshape.83
  20.5 0.0 copy-start.2
  20.6 0.0 copy-start.4
  20.6 0.0 copy-start.5
  20.6 0.4 copy.41
  21.0 1.0 reshape.84.bias_ref
  22.0 0.1 pad.4.clone
  22.1 0.0 collective-permute-done.2
  22.1 0.0 collective-permute-done.3
  22.1 2.0 %pad_maximum_fusion = bf16[34,40,512]{2,1,0:T(8,128)(2,1)S(1)} fusion(bf16[34,1,512]{2,1,0:T(2,128)(2,1)S(1)} %collective-permute-done.3, bf16[34,1,512]{2,1,0:T(2,128)(2,1)S(1)} %collective-permute-done.2, bf16[34,32,512]{2,1,0:T(8,128)(2,1)} %copy-done.7, bf16[40]{0:T(256)(128)(2,1)S(1)} %pad.4.clone), kind=kLoop, calls=%fused_computation.11 | loop fusion | flops 5570560 | bytes 2576464 | tf_op jit(solution)/shard_map/concatenate | solution.py:529
  24.1 0.0 copy-done.2
  24.1 0.0 copy-done.4
  24.2 0.0 copy-done.5
  24.2 0.0 copy-done.1
  24.2 0.0 copy-start.9
  24.2 18.9 %conv_stage.1 = (bf16[1024,2048]{1,0:T(8,128)(2,1)S(1)}, f32[1,2048]{1,0:T(1,128)S(1)}) custom-call(f32[4]{0:T(128)S(1)} %add_convert_fusion.flags, bf16[1360,512]{1,0:T(8,128)(2,1)S(1)} %bitcast.71, f32[1,512]{1,0:T(1,128)S(1)} %bitcast.73, f32[1,512]{1,0:T(1,128)S(1)} %bitcast.74, bf16[512,2048]{1,0:T(8,128)(2,1)S(1)} %copy-done.1, f32[9,2048]{1,0:T(8,128)S(1)} %copy-done.2), custom_call_target="tpu_custom_call" | custom-call | tf_op jit(solution)/shard_map/conv_stage/pallas_call | solution.py:532
  43.0 0.0 copy-start.3
  43.1 0.6 copy-done.3
  43.7 1.9 %copy-done.6 = bf16[1024,2048]{1,0:T(8,128)(2,1)} copy-done((bf16[1024,2048]{1,0:T(8,128)(2,1)}, bf16[1024,2048]{1,0:T(8,128)(2,1)S(1)}, u32[]{:S(2)}) %copy-start.6) | copy-done | bytes 4194328
  45.6 8.1 %axis_sum_row.1.x_ref = f32[16,128]{1,0:T(8,128)} custom-call(f32[16,128]{1,0:T(8,128)} %bitcast.72), custom_call_target="tpu_custom_call" | custom-call | tf_op jit(solution)/shard_map/axis_sum_row/pallas_call | solution.py:210
  53.7 7.6 %axis_sum_col.1 = f32[16,128]{1,0:T(8,128)} custom-call(f32[16,128]{1,0:T(8,128)} %axis_sum_row.1.x_ref), custom_call_target="tpu_custom_call" | custom-call | tf_op jit(solution)/shard_map/axis_sum_col/pallas_call | solution.py:210
  61.3 0.7 broadcast_multiply_fusion
  62.0 1.3 convolution_bitcast_fusion.2
  63.3 1.4 fusion.5
  64.7 0.0 copy-done
  64.7 0.0 copy-done.9
  64.7 4.5 %fusion.2 = bf16[1024,512]{1,0:T(8,128)(2,1)S(1)} fusion(bf16[1024,512]{1,0:T(8,128)(2,1)S(1)} %bitcast.81, bf16[2048,512]{1,0:T(8,128)(2,1)S(1)} %copy-done, bf16[1024,2048]{1,0:T(8,128)(2,1)} %copy-done.6, f32[2048]{0:T(1024)S(1)} %add_divide_fusion), kind=kOutput, calls=%fused_computation.8 | convolution fusion | flops 2155347968 | bytes 8396800 | tf_op jit(solution)/shard_map/dot_general | solution.py:586
  69.3 1.1 fusion.12
  70.3 14.9 %mixer_blocks.3 = bf16[512,512]{1,0:T(8,128)(2,1)} custom-call(bf16[512,512]{1,0:T(8,128)(2,1)} %bitcast.90, f32[1,512]{1,0:T(1,128)} %bitcast.93, f32[2,256,128]{2,1,0:T(8,128)} %reshape.79.bias_ref, f32[1,512]{1,0:T(1,128)} %bitcast.95, bf16[512,1536]{1,0:T(8,128)(2,1)} %proj_hbm.6, bf16[512,512]{1,0:T(8,128)(2,1)} %out_hbm.6, bf16[512,2048]{1,0:T(8,128)(2,1)} %up_hbm.6, ...), custom_call_target="tpu_custom_call" | custom-call | flops 12884901888 | bytes 12582912 | tf_op jit(solution)/shard_map/mixer_blocks/pallas_call | solution.py:367
  85.3 1.9 %copy.31 = bf16[8,4,2,1,8,512]{5,4,2,1,0,3:T(8,128)(2,1)} copy(bf16[8,4,2,1,8,512]{5,4,1,0,2,3:T(8,128)(2,1)} %bitcast.88) | data formatting | bytes 1048576 | tf_op jit(solution)/shard_map/transpose | solution.py:437
  87.2 4.8 %all-to-all-start.2 = ((bf16[32,16,512]{2,1,0:T(8,128)(2,1)}), bf16[32,16,512]{2,1,0:T(8,128)(2,1)S(1)}, u32[]{:S(2)}, u32[]{:S(2)}) async-start(bf16[32,16,512]{2,1,0:T(8,128)(2,1)} %bitcast.35), calls=%async_computation.2 | async-start | bytes 1048576 | tf_op jit(solution)/shard_map/all_to_all | solution.py:440
  92.0 14.9 %mixer_blocks.2 = bf16[512,512]{1,0:T(8,128)(2,1)} custom-call(bf16[512,512]{1,0:T(8,128)(2,1)} %bitcast.89, f32[1,512]{1,0:T(1,128)} %bitcast.94, f32[2,256,128]{2,1,0:T(8,128)} %reshape.79.bias_ref, f32[1,512]{1,0:T(1,128)} %bitcast.96, bf16[512,1536]{1,0:T(8,128)(2,1)} %proj_hbm.6, bf16[512,512]{1,0:T(8,128)(2,1)} %out_hbm.6, bf16[512,2048]{1,0:T(8,128)(2,1)} %up_hbm.6, ...), custom_call_target="tpu_custom_call" | custom-call | flops 12884901888 | bytes 12582912 | tf_op jit(solution)/shard_map/mixer_blocks/pallas_call | solution.py:367
  106.9 1.9 %copy.27 = bf16[8,4,2,1,8,512]{5,4,2,1,0,3:T(8,128)(2,1)} copy(bf16[8,4,2,1,8,512]{5,4,1,0,2,3:T(8,128)(2,1)} %bitcast.87) | data formatting | bytes 1048576 | tf_op jit(solution)/shard_map/transpose | solution.py:437
  108.8 0.0 all-to-all-done.2
  108.8 5.6 %all-to-all-start = ((bf16[32,16,512]{2,1,0:T(8,128)(2,1)}), bf16[32,16,512]{2,1,0:T(8,128)(2,1)S(1)}, u32[]{:S(2)}, u32[]{:S(2)}) async-start(bf16[32,16,512]{2,1,0:T(8,128)(2,1)} %bitcast.22), calls=%async_computation | async-start | bytes 1048576 | tf_op jit(solution)/shard_map/all_to_all | solution.py:440
  114.5 14.9 %mixer_strided.3 = bf16[512,512]{1,0:T(8,128)(2,1)} custom-call(bf16[512,512]{1,0:T(8,128)(2,1)} %bitcast.83, f32[1,512]{1,0:T(1,128)} %bitcast.97, f32[2,256,128]{2,1,0:T(8,128)} %reshape.84.bias_ref, f32[1,512]{1,0:T(1,128)} %bitcast.99, bf16[512,1536]{1,0:T(8,128)(2,1)} %proj_hbm.7, bf16[512,512]{1,0:T(8,128)(2,1)} %out_hbm.7, bf16[512,2048]{1,0:T(8,128)(2,1)} %up_hbm.7, ...), custom_call_target="tpu_custom_call" | custom-call | flops 12884901888 | bytes 12582912 | tf_op jit(solution)/shard_map/mixer_strided/pallas_call | solution.py:367
  129.4 1.3 all-to-all-done
  130.7 4.6 %all-to-all-start.3 = ((bf16[32,16,512]{2,1,0:T(8,128)(2,1)}), bf16[32,16,512]{2,1,0:T(8,128)(2,1)S(1)}, u32[]{:S(2)}, u32[]{:S(2)}) async-start(bf16[32,16,512]{2,1,0:T(8,128)(2,1)} %bitcast.85), calls=%async_computation.3 | async-start | bytes 1048576 | tf_op jit(solution)/shard_map/all_to_all | solution.py:442
  135.3 0.0 copy-done.11
  135.3 14.9 %mixer_strided.2 = bf16[512,512]{1,0:T(8,128)(2,1)} custom-call(bf16[512,512]{1,0:T(8,128)(2,1)} %bitcast.84, f32[1,512]{1,0:T(1,128)} %bitcast.98, f32[2,256,128]{2,1,0:T(8,128)} %reshape.84.bias_ref, f32[1,512]{1,0:T(1,128)} %bitcast.100, bf16[512,1536]{1,0:T(8,128)(2,1)} %proj_hbm.7, bf16[512,512]{1,0:T(8,128)(2,1)} %out_hbm.7, bf16[512,2048]{1,0:T(8,128)(2,1)} %up_hbm.7, ...), custom_call_target="tpu_custom_call" | custom-call | flops 12884901888 | bytes 12582912 | tf_op jit(solution)/shard_map/mixer_strided/pallas_call | solution.py:367
  150.2 1.3 all-to-all-done.3
  151.5 4.6 %all-to-all-start.1 = ((bf16[32,16,512]{2,1,0:T(8,128)(2,1)}), bf16[32,16,512]{2,1,0:T(8,128)(2,1)S(1)}, u32[]{:S(2)}, u32[]{:S(2)}) async-start(bf16[32,16,512]{2,1,0:T(8,128)(2,1)} %bitcast.86), calls=%async_computation.1 | async-start | bytes 1048576 | tf_op jit(solution)/shard_map/all_to_all | solution.py:442
  156.1 0.9 copy.39
  157.0 15.4 %all-to-all-done.1 = bf16[32,16,512]{2,1,0:T(8,128)(2,1)S(1)} async-done(((bf16[32,16,512]{2,1,0:T(8,128)(2,1)}), bf16[32,16,512]{2,1,0:T(8,128)(2,1)S(1)}, u32[]{:S(2)}, u32[]{:S(2)}) %all-to-all-start.1) | async-done | bytes 524320 | tf_op jit(solution)/shard_map/all_to_all | solution.py:442
  172.4 2.1 %pad_maximum_fusion.1 = bf16[2,2,8,32,512]{4,3,2,1,0:T(8,128)(2,1)} fusion(bf16[2,1,8,32,512]{4,3,2,1,0:T(8,128)(2,1)} %bitcast.79, bf16[2,1,8,32,512]{4,3,2,1,0:T(8,128)(2,1)S(1)} %bitcast.80), kind=kLoop, calls=%fused_computation.13 | loop fusion | flops 524288 | bytes 2097152 | tf_op jit(solution)/shard_map/stack | solution.py:450
  (11 shorter events, 0.1 us)
Async XLA Ops:
  0.0 64.7 %copy-start = (bf16[2048,512]{1,0:T(8,128)(2,1)S(1)}, bf16[2048,512]{1,0:T(8,128)(2,1)}, u32[]{:S(2)}) copy-start(bf16[2048,512]{1,0:T(8,128)(2,1)} %param.31) | copy-start | bytes 6291460
  0.0 12.1 %copy-start.8 = (bf16[32,32,512]{2,1,0:T(8,128)(2,1)S(1)}, bf16[32,32,512]{2,1,0:T(8,128)(2,1)}, u32[]{:S(2)}) copy-start(bf16[32,32,512]{2,1,0:T(8,128)(2,1)} %param.24) | copy-start | bytes 3145732
  0.9 11.1 %collective-permute-start = (bf16[1,32,512]{2,1,0:T(8,128)(2,1)S(1)}, bf16[1,32,512]{2,1,0:T(8,128)(2,1)S(1)}, u32[]{:S(2)}, u32[]{:S(2)}) collective-permute-start(bf16[1,32,512]{2,1,0:T(8,128)(2,1)S(1)} %get-tuple-element.14), channel_id=1, source_target_pairs={{0,8},{8,16},{16,24},{1,9},{9,17},{17,25},{2,10},{10,18},{18,26},{... | collective-permute-start | bytes 98312 | tf_op jit(solution)/shard_map/ppermute | solution.py:22
  5.9 6.3 %collective-permute-start.1 = (bf16[1,32,512]{2,1,0:T(8,128)(2,1)S(1)}, bf16[1,32,512]{2,1,0:T(8,128)(2,1)S(1)}, u32[]{:S(2)}, u32[]{:S(2)}) collective-permute-start(bf16[1,32,512]{2,1,0:T(8,128)(2,1)S(1)} %get-tuple-element.13), channel_id=1, source_target_pairs={{8,0},{16,8},{24,16},{9,1},{17,9},{25,17},{10,2},{18,10},{26,18},{... | collective-permute-start | bytes 98312 | tf_op jit(solution)/shard_map/ppermute | solution.py:24
  12.2 5.4 %copy-start.7 = (bf16[34,32,512]{2,1,0:T(8,128)(2,1)}, bf16[34,32,512]{2,1,0:T(8,128)(2,1)S(1)}, u32[]{:S(2)}) copy-start(bf16[34,32,512]{2,1,0:T(8,128)(2,1)S(1)} %constant_dynamic-update-slice_fusion) | copy-start | bytes 3342340
  13.1 9.0 %collective-permute-start.2 = (bf16[34,1,512]{2,1,0:T(2,128)(2,1)}, bf16[34,1,512]{2,1,0:T(2,128)(2,1)S(1)}, u32[]{:S(2)}, u32[]{:S(2)}) collective-permute-start(bf16[34,1,512]{2,1,0:T(2,128)(2,1)} %get-tuple-element.9), channel_id=1, source_target_pairs={{1,0},{2,1},{3,2},{4,3},{5,4},{6,5},{7,6},{9,8},{10,9},{11,10},{12... | collective-permute-start | bytes 104456 | tf_op jit(solution)/shard_map/ppermute | solution.py:527
  14.4 7.7 %collective-permute-start.3 = (bf16[34,1,512]{2,1,0:T(2,128)(2,1)}, bf16[34,1,512]{2,1,0:T(2,128)(2,1)S(1)}, u32[]{:S(2)}, u32[]{:S(2)}) collective-permute-start(bf16[34,1,512]{2,1,0:T(2,128)(2,1)} %get-tuple-element.10), channel_id=1, source_target_pairs={{0,1},{1,2},{2,3},{3,4},{4,5},{5,6},{6,7},{8,9},{9,10},{10,11},{11... | collective-permute-start | bytes 104456 | tf_op jit(solution)/shard_map/ppermute | solution.py:526
  20.5 3.6 %copy-start.2 = (f32[9,2048]{1,0:T(8,128)S(1)}, f32[9,2048]{1,0:T(8,128)}, u32[]{:S(2)}) copy-start(f32[9,2048]{1,0:T(8,128)} %taps_ref.1) | copy-start | bytes 221188
  20.6 3.6 %copy-start.4 = (f32[512]{0:T(512)S(1)}, f32[512]{0:T(512)}, u32[]{:S(2)}) copy-start(f32[512]{0:T(512)} %param.25) | copy-start | bytes 6148
  20.6 3.6 %copy-start.5 = (f32[512]{0:T(512)S(1)}, f32[512]{0:T(512)}, u32[]{:S(2)}) copy-start(f32[512]{0:T(512)} %param.26) | copy-start | bytes 6148
  22.0 2.1 %copy-start.1 = (bf16[512,2048]{1,0:T(8,128)(2,1)S(1)}, bf16[512,2048]{1,0:T(8,128)(2,1)}, u32[]{:S(2)}) copy-start(bf16[512,2048]{1,0:T(8,128)(2,1)} %expand_ref.1) | copy-start | bytes 6291460
  24.2 40.6 %copy-start.9 = (bf16[32,32,512]{2,1,0:T(8,128)(2,1)S(1)}, bf16[32,32,512]{2,1,0:T(8,128)(2,1)}, u32[]{:S(2)}) copy-start(bf16[32,32,512]{2,1,0:T(8,128)(2,1)} %param.24) | copy-start | bytes 3145732
  43.0 0.6 copy-start.3
  43.6 1.9 %copy-start.6 = (bf16[1024,2048]{1,0:T(8,128)(2,1)}, bf16[1024,2048]{1,0:T(8,128)(2,1)S(1)}, u32[]{:S(2)}) copy-start(bf16[1024,2048]{1,0:T(8,128)(2,1)S(1)} %get-tuple-element.7) | copy-start | bytes 12582916
  87.2 21.6 %all-to-all-start.2 = ((bf16[32,16,512]{2,1,0:T(8,128)(2,1)}), bf16[32,16,512]{2,1,0:T(8,128)(2,1)S(1)}, u32[]{:S(2)}, u32[]{:S(2)}) async-start(bf16[32,16,512]{2,1,0:T(8,128)(2,1)} %bitcast.35), calls=%async_computation.2 | async-start | bytes 1048576 | tf_op jit(solution)/shard_map/all_to_all | solution.py:440
  108.8 5.6 %copy-start.10 = (bf16[32,16,512]{2,1,0:T(8,128)(2,1)}, bf16[32,16,512]{2,1,0:T(8,128)(2,1)S(1)}, u32[]{:S(2)}) copy-start(bf16[32,16,512]{2,1,0:T(8,128)(2,1)S(1)} %all-to-all-done.2) | copy-start | bytes 1572868
  108.8 21.9 %all-to-all-start = ((bf16[32,16,512]{2,1,0:T(8,128)(2,1)}), bf16[32,16,512]{2,1,0:T(8,128)(2,1)S(1)}, u32[]{:S(2)}, u32[]{:S(2)}) async-start(bf16[32,16,512]{2,1,0:T(8,128)(2,1)} %bitcast.22), calls=%async_computation | async-start | bytes 1048576 | tf_op jit(solution)/shard_map/all_to_all | solution.py:440
  130.7 4.6 %copy-start.11 = (bf16[32,16,512]{2,1,0:T(8,128)(2,1)}, bf16[32,16,512]{2,1,0:T(8,128)(2,1)S(1)}, u32[]{:S(2)}) copy-start(bf16[32,16,512]{2,1,0:T(8,128)(2,1)S(1)} %all-to-all-done) | copy-start | bytes 1572868
  130.7 20.8 %all-to-all-start.3 = ((bf16[32,16,512]{2,1,0:T(8,128)(2,1)}), bf16[32,16,512]{2,1,0:T(8,128)(2,1)S(1)}, u32[]{:S(2)}, u32[]{:S(2)}) async-start(bf16[32,16,512]{2,1,0:T(8,128)(2,1)} %bitcast.85), calls=%async_computation.3 | async-start | bytes 1048576 | tf_op jit(solution)/shard_map/all_to_all | solution.py:442
  151.5 20.8 %all-to-all-start.1 = ((bf16[32,16,512]{2,1,0:T(8,128)(2,1)}), bf16[32,16,512]{2,1,0:T(8,128)(2,1)S(1)}, u32[]{:S(2)}, u32[]{:S(2)}) async-start(bf16[32,16,512]{2,1,0:T(8,128)(2,1)} %bitcast.86), calls=%async_computation.1 | async-start | bytes 1048576 | tf_op jit(solution)/shard_map/all_to_all | solution.py:442

commit v3 on v2

--- a/solution.py
+++ b/solution.py
@@ -217,7 +217,9 @@
             pltpu.SemaphoreType.DMA((count - 1,)),
             pltpu.SemaphoreType.DMA((count - 1,)),
         ],
-        compiler_params=pltpu.CompilerParams(collective_id=collective_id, has_side_effects=True),
+        compiler_params=pltpu.CompilerParams(
+            collective_id=collective_id, has_side_effects=True, vmem_limit_bytes=4 * 1024 * 1024
+        ),
         name="axis_sum_" + axis,
     )(values)
 
@@ -248,9 +250,10 @@
             ((proj_hbm, proj_ref), (out_hbm, out_w_ref), (up_hbm, up_ref), (down_hbm, down_ref))
         )
     ]
-    for move in moves:
+    moves[0].start()
+    moves[0].wait()
+    for move in moves[1:]:
         move.start()
-    moves[0].wait()
     chunk = 256
 
     def project(step, carry):
@@ -313,7 +316,7 @@
             )
             scores = (scores * scale + bias_ref[group]).reshape(per_slab, tokens, 2 * tokens)
             weights = jnp.exp(scores - jnp.max(scores, axis=1, keepdims=True))
-            shares = weights / jnp.sum(weights, axis=1, keepdims=True)
+            shares = weights * (1.0 / jnp.sum(weights, axis=1, keepdims=True))
             shares = shares.reshape(per_slab * tokens, 2 * tokens).astype(jnp.bfloat16)
             mixed = lax.dot_general(
                 shares, block_v, (((0,), (0,)), ((), ())), preferred_element_type=jnp.float32
@@ -541,7 +544,7 @@
             pltpu.VMEM(ext.shape, jnp.bfloat16),
             pltpu.VMEM((row_count + 2, col_count + PAD, block), jnp.float32),
         ],
-        compiler_params=pltpu.CompilerParams(vmem_limit_bytes=40 * 1024 * 1024),
+        compiler_params=pltpu.CompilerParams(vmem_limit_bytes=20 * 1024 * 1024),
         name="conv_stage",
     )(flags, ext, conv_scale[None], conv_shift[None], expand_weight, depth_kernel)
 

time: 176 us -> 166 us (0.943)
  matrix products: 12.1 us -> 7.82 us
  local copies, waits for them, and re-layouts: 14.6 us -> 12.1 us
  Pallas kernels: 94.2 us -> 91.8 us
    unnamed x26, local copies, waits for them, and re-layouts: 2.69 us -> 0.16 us
    pallas_call x2, Pallas kernels: 15.7 us -> 13.2 us  [axis_sum(): pl.pallas_call(functools.partial(axis_sum_kernel, axis, count), out_shape...]
    dot_general x1, matrix products: 4.52 us -> 2.34 us  [per_device(): jnp.dot(gated, project_weight, preferred_element_type=jnp.float32)]
  transfers between devices with their start and end apart: 8 -> 8, of which waited for: 3 -> 3; matrix products, arithmetic and copies ran while one was open for 7% -> 7% of each run, Pallas kernels for 26% -> 27%
where the time goes in v3:
time: 166 us; the launch traced here: 165 us
  Pallas kernels  91.8 us (55%)
  starting transfers between devices  30.9 us (19%)
  waiting for transfers between devices  17.9 us (11%)
  local copies, waits for them, and re-layouts  12.1 us (7%)
  matrix products  7.82 us (5%)
  other arithmetic  4.27 us (3%)
    pallas_call x4, Pallas kernels, mixer(): pl.pallas_call(functools.partial(mixer_kernel, layout, feats // heads_cou...  59.7 us
    pallas_call x1, Pallas kernels, depthwise_stage(): pl.pallas_call(functools.partial(conv_kernel, row_count, col_count), out_...  18.9 us
    all_to_all x2, waiting for transfers between devices, split_sublayers(): lax.all_to_all(out.reshape(devices, -1, feats), ('row', 'col'), split_axi...  16.6 us
    pallas_call x2, Pallas kernels, axis_sum(): pl.pallas_call(functools.partial(axis_sum_kernel, axis, count), out_shape...  13.2 us
    all_to_all x2, starting transfers between devices, split_sublayers(): lax.all_to_all(sent, ('row', 'col'), split_axis=0, concat_axis=0, tiled=T...  10.5 us
    all_to_all x2, starting transfers between devices, split_sublayers(): lax.all_to_all(out.reshape(devices, -1, feats), ('row', 'col'), split_axi...  9.15 us
    ppermute x1, starting transfers between devices, extended(): lax.ppermute(tail, axis, [(i, (i + 1) % count) for i in range(ends)])  4.99 us
    dot_general x2, matrix products, key_major_bias(): spread = jnp.dot(table, chosen, precision=lax.Precision.HIGHEST)  4.84 us
  transfers between devices with their start and end apart: 8, of which 3 were waited for; matrix products, arithmetic and copies ran while one was open for 7% of the time, Pallas kernels for 27%

profile of v3, /device:TPU:0, one launch (start us, length us, event | category | flops | bytes accessed | tf_op | source)
XLA Modules:
  0.0 165.2 jit_solution(9568147631204398551)
XLA Ops:
  0.0 0.0 copy-start
  0.0 0.9 fusion.13
  0.9 5.0 %collective-permute-start = (bf16[1,32,512]{2,1,0:T(8,128)(2,1)S(1)}, bf16[1,32,512]{2,1,0:T(8,128)(2,1)S(1)}, u32[]{:S(2)}, u32[]{:S(2)}) collective-permute-start(bf16[1,32,512]{2,1,0:T(8,128)(2,1)S(1)} %get-tuple-element.14), channel_id=1, source_target_pairs={{0,8},{8,16},{16,24},{1,9},{9,17},{17,25},{2,10},{10,18},{18,26},{... | collective-permute-start | bytes 98312 | tf_op jit(solution)/shard_map/ppermute | solution.py:22
  5.9 1.3 collective-permute-start.1
  7.2 2.8 %convolution_bitcast_fusion.1 = f32[16,4096]{1,0:T(8,128)} fusion(f32[16,225]{1,0:T(8,128)} %param.35, s32[4096]{0:T(1024)} %constant.27.clone), kind=kOutput, calls=%fused_computation.2 | convolution fusion | flops 177868800 | bytes 292928 | tf_op jit(solution)/shard_map/dot_general | solution.py:401
  10.0 2.1 %convolution_bitcast_fusion = f32[16,4096]{1,0:T(8,128)S(1)} fusion(f32[16,225]{1,0:T(8,128)} %param.42, s32[4096]{0:T(1024)} %constant.28.clone), kind=kOutput, calls=%fused_computation.1 | convolution fusion | flops 177868800 | bytes 292928 | tf_op jit(solution)/shard_map/dot_general | solution.py:401
  12.1 0.0 collective-permute-done
  12.1 0.0 copy-done.6
  12.1 0.1 constant_dynamic-update-slice_fusion.1
  12.2 0.0 collective-permute-done.1
  12.2 0.0 copy-start.5
  12.2 0.9 fusion.11
  13.2 1.3 collective-permute-start.2
  14.4 3.7 %collective-permute-start.3 = (bf16[34,1,512]{2,1,0:T(2,128)(2,1)}, bf16[34,1,512]{2,1,0:T(2,128)(2,1)}, u32[]{:S(2)}, u32[]{:S(2)}) collective-permute-start(bf16[34,1,512]{2,1,0:T(2,128)(2,1)} %get-tuple-element.10), channel_id=1, source_target_pairs={{0,1},{1,2},{2,3},{3,4},{4,5},{5,6},{6,7},{8,9},{9,10},{10,11},{11... | collective-permute-start | bytes 104456 | tf_op jit(solution)/shard_map/ppermute | solution.py:529
  18.1 0.0 copy-done.5
  18.1 0.1 add_convert_fusion.flags
  18.2 1.1 reshape.78
  19.3 0.4 copy.42
  19.8 1.0 reshape.79.bias_ref
  20.8 0.2 reshape.83
  21.0 0.0 copy-start.2
  21.0 0.0 copy-start.3
  21.0 0.0 copy-start.4
  21.0 0.4 copy.41
  21.4 1.0 reshape.84.bias_ref
  22.5 0.1 pad.4.clone
  22.6 0.0 collective-permute-done.2
  22.6 0.0 collective-permute-done.3
  22.6 2.1 %pad_maximum_fusion = bf16[34,40,512]{2,1,0:T(8,128)(2,1)S(1)} fusion(bf16[34,1,512]{2,1,0:T(2,128)(2,1)} %collective-permute-done.3, bf16[34,1,512]{2,1,0:T(2,128)(2,1)} %collective-permute-done.2, bf16[34,32,512]{2,1,0:T(8,128)(2,1)} %copy-done.5, bf16[40]{0:T(256)(128)(2,1)S(1)} %pad.4.clone), kind=kLoop, calls=%fused_computation.11 | loop fusion | flops 5570560 | bytes 2576464 | tf_op jit(solution)/shard_map/concatenate | solution.py:532
  24.6 0.0 copy-start.8
  24.6 0.0 copy-done.2
  24.6 0.0 copy-done.3
  24.7 0.0 copy-done.4
  24.7 0.0 copy-done.1
  24.7 0.0 copy-start.9
  24.7 0.0 copy-start.7
  24.7 18.9 %conv_stage.1 = (bf16[1024,2048]{1,0:T(8,128)(2,1)S(1)}, f32[1,2048]{1,0:T(1,128)S(1)}) custom-call(f32[4]{0:T(128)S(1)} %add_convert_fusion.flags, bf16[1360,512]{1,0:T(8,128)(2,1)S(1)} %bitcast.71, f32[1,512]{1,0:T(1,128)S(1)} %bitcast.73, f32[1,512]{1,0:T(1,128)S(1)} %bitcast.74, bf16[512,2048]{1,0:T(8,128)(2,1)S(1)} %copy-done.1, f32[9,2048]{1,0:T(8,128)S(1)} %copy-done.2), custom_call_target="tpu_custom_call" | custom-call | tf_op jit(solution)/shard_map/conv_stage/pallas_call | solution.py:535
  43.6 6.9 %axis_sum_row.1.x_ref = f32[16,128]{1,0:T(8,128)S(1)} custom-call(f32[16,128]{1,0:T(8,128)S(1)} %bitcast.72), custom_call_target="tpu_custom_call" | custom-call | tf_op jit(solution)/shard_map/axis_sum_row/pallas_call | solution.py:210
  50.4 6.4 %axis_sum_col.1 = f32[16,128]{1,0:T(8,128)S(1)} custom-call(f32[16,128]{1,0:T(8,128)S(1)} %axis_sum_row.1.x_ref), custom_call_target="tpu_custom_call" | custom-call | tf_op jit(solution)/shard_map/axis_sum_col/pallas_call | solution.py:210
  56.8 0.0 copy-done.8
  56.8 0.3 convolution_bitcast_fusion.2
  57.1 0.0 copy-done.9
  57.1 0.3 fusion.5
  57.5 0.0 copy-done
  57.5 0.0 copy-done.7
  57.5 2.3 %fusion.2 = bf16[1024,512]{1,0:T(8,128)(2,1)S(1)} fusion(bf16[1024,512]{1,0:T(8,128)(2,1)S(1)} %bitcast.81, bf16[2048,512]{1,0:T(8,128)(2,1)S(1)} %copy-done, bf16[1024,2048]{1,0:T(8,128)(2,1)S(1)} %get-tuple-element.7, f32[2048]{0:T(1024)S(1)} %add_divide_fusion), kind=kOutput, calls=%fused_computation.8 | convolution fusion | flops 2155347968 | bytes 8396800 | tf_op jit(solution)/shard_map/dot_general | solution.py:589
  59.9 1.1 fusion.12
  60.9 14.9 %mixer_blocks.3 = bf16[512,512]{1,0:T(8,128)(2,1)} custom-call(bf16[512,512]{1,0:T(8,128)(2,1)} %bitcast.90, f32[1,512]{1,0:T(1,128)} %bitcast.93, f32[2,256,128]{2,1,0:T(8,128)} %reshape.79.bias_ref, f32[1,512]{1,0:T(1,128)} %bitcast.95, bf16[512,1536]{1,0:T(8,128)(2,1)} %proj_hbm.6, bf16[512,512]{1,0:T(8,128)(2,1)} %out_hbm.6, bf16[512,2048]{1,0:T(8,128)(2,1)} %up_hbm.6, ...), custom_call_target="tpu_custom_call" | custom-call | flops 12884901888 | bytes 12582912 | tf_op jit(solution)/shard_map/mixer_blocks/pallas_call | solution.py:370
  75.8 1.9 %copy.31 = bf16[8,4,2,1,8,512]{5,4,2,1,0,3:T(8,128)(2,1)} copy(bf16[8,4,2,1,8,512]{5,4,1,0,2,3:T(8,128)(2,1)} %bitcast.88) | data formatting | bytes 1048576 | tf_op jit(solution)/shard_map/transpose | solution.py:440
  77.8 4.9 %all-to-all-start.2 = ((bf16[32,16,512]{2,1,0:T(8,128)(2,1)}), bf16[32,16,512]{2,1,0:T(8,128)(2,1)S(1)}, u32[]{:S(2)}, u32[]{:S(2)}) async-start(bf16[32,16,512]{2,1,0:T(8,128)(2,1)} %bitcast.35), calls=%async_computation.2 | async-start | bytes 1048576 | tf_op jit(solution)/shard_map/all_to_all | solution.py:443
  82.7 14.9 %mixer_blocks.2 = bf16[512,512]{1,0:T(8,128)(2,1)} custom-call(bf16[512,512]{1,0:T(8,128)(2,1)} %bitcast.89, f32[1,512]{1,0:T(1,128)} %bitcast.94, f32[2,256,128]{2,1,0:T(8,128)} %reshape.79.bias_ref, f32[1,512]{1,0:T(1,128)} %bitcast.96, bf16[512,1536]{1,0:T(8,128)(2,1)} %proj_hbm.6, bf16[512,512]{1,0:T(8,128)(2,1)} %out_hbm.6, bf16[512,2048]{1,0:T(8,128)(2,1)} %up_hbm.6, ...), custom_call_target="tpu_custom_call" | custom-call | flops 12884901888 | bytes 12582912 | tf_op jit(solution)/shard_map/mixer_blocks/pallas_call | solution.py:370
  97.6 1.9 %copy.27 = bf16[8,4,2,1,8,512]{5,4,2,1,0,3:T(8,128)(2,1)} copy(bf16[8,4,2,1,8,512]{5,4,1,0,2,3:T(8,128)(2,1)} %bitcast.87) | data formatting | bytes 1048576 | tf_op jit(solution)/shard_map/transpose | solution.py:440
  99.5 0.0 all-to-all-done.2
  99.5 5.6 %all-to-all-start = ((bf16[32,16,512]{2,1,0:T(8,128)(2,1)}), bf16[32,16,512]{2,1,0:T(8,128)(2,1)S(1)}, u32[]{:S(2)}, u32[]{:S(2)}) async-start(bf16[32,16,512]{2,1,0:T(8,128)(2,1)} %bitcast.22), calls=%async_computation | async-start | bytes 1048576 | tf_op jit(solution)/shard_map/all_to_all | solution.py:443
  105.2 0.0 copy-done.10
  105.2 14.9 %mixer_strided.3 = bf16[512,512]{1,0:T(8,128)(2,1)} custom-call(bf16[512,512]{1,0:T(8,128)(2,1)} %bitcast.83, f32[1,512]{1,0:T(1,128)} %bitcast.97, f32[2,256,128]{2,1,0:T(8,128)} %reshape.84.bias_ref, f32[1,512]{1,0:T(1,128)} %bitcast.99, bf16[512,1536]{1,0:T(8,128)(2,1)} %proj_hbm.7, bf16[512,512]{1,0:T(8,128)(2,1)} %out_hbm.7, bf16[512,2048]{1,0:T(8,128)(2,1)} %up_hbm.7, ...), custom_call_target="tpu_custom_call" | custom-call | flops 12884901888 | bytes 12582912 | tf_op jit(solution)/shard_map/mixer_strided/pallas_call | solution.py:370
  120.1 1.3 all-to-all-done
  121.4 4.6 %all-to-all-start.3 = ((bf16[32,16,512]{2,1,0:T(8,128)(2,1)}), bf16[32,16,512]{2,1,0:T(8,128)(2,1)S(1)}, u32[]{:S(2)}, u32[]{:S(2)}) async-start(bf16[32,16,512]{2,1,0:T(8,128)(2,1)} %bitcast.85), calls=%async_computation.3 | async-start | bytes 1048576 | tf_op jit(solution)/shard_map/all_to_all | solution.py:445
  126.0 14.9 %mixer_strided.2 = bf16[512,512]{1,0:T(8,128)(2,1)} custom-call(bf16[512,512]{1,0:T(8,128)(2,1)} %bitcast.84, f32[1,512]{1,0:T(1,128)} %bitcast.98, f32[2,256,128]{2,1,0:T(8,128)} %reshape.84.bias_ref, f32[1,512]{1,0:T(1,128)} %bitcast.100, bf16[512,1536]{1,0:T(8,128)(2,1)} %proj_hbm.7, bf16[512,512]{1,0:T(8,128)(2,1)} %out_hbm.7, bf16[512,2048]{1,0:T(8,128)(2,1)} %up_hbm.7, ...), custom_call_target="tpu_custom_call" | custom-call | flops 12884901888 | bytes 12582912 | tf_op jit(solution)/shard_map/mixer_strided/pallas_call | solution.py:370
  140.9 1.3 all-to-all-done.3
  142.2 4.6 %all-to-all-start.1 = ((bf16[32,16,512]{2,1,0:T(8,128)(2,1)}), bf16[32,16,512]{2,1,0:T(8,128)(2,1)S(1)}, u32[]{:S(2)}, u32[]{:S(2)}) async-start(bf16[32,16,512]{2,1,0:T(8,128)(2,1)} %bitcast.86), calls=%async_computation.1 | async-start | bytes 1048576 | tf_op jit(solution)/shard_map/all_to_all | solution.py:445
  146.8 0.9 copy.39
  147.7 15.4 %all-to-all-done.1 = bf16[32,16,512]{2,1,0:T(8,128)(2,1)S(1)} async-done(((bf16[32,16,512]{2,1,0:T(8,128)(2,1)}), bf16[32,16,512]{2,1,0:T(8,128)(2,1)S(1)}, u32[]{:S(2)}, u32[]{:S(2)}) %all-to-all-start.1) | async-done | bytes 524320 | tf_op jit(solution)/shard_map/all_to_all | solution.py:445
  163.1 2.1 %pad_maximum_fusion.1 = bf16[2,2,8,32,512]{4,3,2,1,0:T(8,128)(2,1)} fusion(bf16[2,1,8,32,512]{4,3,2,1,0:T(8,128)(2,1)} %bitcast.79, bf16[2,1,8,32,512]{4,3,2,1,0:T(8,128)(2,1)S(1)} %bitcast.80), kind=kLoop, calls=%fused_computation.13 | loop fusion | flops 524288 | bytes 2097152 | tf_op jit(solution)/shard_map/stack | solution.py:453
  (11 shorter events, 0.1 us)
Async XLA Ops:
  0.0 57.5 %copy-start = (bf16[2048,512]{1,0:T(8,128)(2,1)S(1)}, bf16[2048,512]{1,0:T(8,128)(2,1)}, u32[]{:S(2)}) copy-start(bf16[2048,512]{1,0:T(8,128)(2,1)} %param.31) | copy-start | bytes 6291460
  0.0 12.1 %copy-start.6 = (bf16[32,32,512]{2,1,0:T(8,128)(2,1)S(1)}, bf16[32,32,512]{2,1,0:T(8,128)(2,1)}, u32[]{:S(2)}) copy-start(bf16[32,32,512]{2,1,0:T(8,128)(2,1)} %param.24) | copy-start | bytes 3145732
  0.9 11.1 %collective-permute-start = (bf16[1,32,512]{2,1,0:T(8,128)(2,1)S(1)}, bf16[1,32,512]{2,1,0:T(8,128)(2,1)S(1)}, u32[]{:S(2)}, u32[]{:S(2)}) collective-permute-start(bf16[1,32,512]{2,1,0:T(8,128)(2,1)S(1)} %get-tuple-element.14), channel_id=1, source_target_pairs={{0,8},{8,16},{16,24},{1,9},{9,17},{17,25},{2,10},{10,18},{18,26},{... | collective-permute-start | bytes 98312 | tf_op jit(solution)/shard_map/ppermute | solution.py:22
  5.9 6.3 %collective-permute-start.1 = (bf16[1,32,512]{2,1,0:T(8,128)(2,1)S(1)}, bf16[1,32,512]{2,1,0:T(8,128)(2,1)S(1)}, u32[]{:S(2)}, u32[]{:S(2)}) collective-permute-start(bf16[1,32,512]{2,1,0:T(8,128)(2,1)S(1)} %get-tuple-element.13), channel_id=1, source_target_pairs={{8,0},{16,8},{24,16},{9,1},{17,9},{25,17},{10,2},{18,10},{26,18},{... | collective-permute-start | bytes 98312 | tf_op jit(solution)/shard_map/ppermute | solution.py:24
  12.2 5.9 %copy-start.5 = (bf16[34,32,512]{2,1,0:T(8,128)(2,1)}, bf16[34,32,512]{2,1,0:T(8,128)(2,1)S(1)}, u32[]{:S(2)}) copy-start(bf16[34,32,512]{2,1,0:T(8,128)(2,1)S(1)} %constant_dynamic-update-slice_fusion) | copy-start | bytes 3342340
  13.2 9.4 %collective-permute-start.2 = (bf16[34,1,512]{2,1,0:T(2,128)(2,1)}, bf16[34,1,512]{2,1,0:T(2,128)(2,1)}, u32[]{:S(2)}, u32[]{:S(2)}) collective-permute-start(bf16[34,1,512]{2,1,0:T(2,128)(2,1)} %get-tuple-element.9), channel_id=1, source_target_pairs={{1,0},{2,1},{3,2},{4,3},{5,4},{6,5},{7,6},{9,8},{10,9},{11,10},{12... | collective-permute-start | bytes 104456 | tf_op jit(solution)/shard_map/ppermute | solution.py:530
  14.4 8.1 %collective-permute-start.3 = (bf16[34,1,512]{2,1,0:T(2,128)(2,1)}, bf16[34,1,512]{2,1,0:T(2,128)(2,1)}, u32[]{:S(2)}, u32[]{:S(2)}) collective-permute-start(bf16[34,1,512]{2,1,0:T(2,128)(2,1)} %get-tuple-element.10), channel_id=1, source_target_pairs={{0,1},{1,2},{2,3},{3,4},{4,5},{5,6},{6,7},{8,9},{9,10},{10,11},{11... | collective-permute-start | bytes 104456 | tf_op jit(solution)/shard_map/ppermute | solution.py:529
  21.0 3.7 %copy-start.2 = (f32[9,2048]{1,0:T(8,128)S(1)}, f32[9,2048]{1,0:T(8,128)}, u32[]{:S(2)}) copy-start(f32[9,2048]{1,0:T(8,128)} %taps_ref.1) | copy-start | bytes 221188
  21.0 3.7 %copy-start.3 = (f32[512]{0:T(512)S(1)}, f32[512]{0:T(512)}, u32[]{:S(2)}) copy-start(f32[512]{0:T(512)} %param.25) | copy-start | bytes 6148
  21.0 3.7 %copy-start.4 = (f32[512]{0:T(512)S(1)}, f32[512]{0:T(512)}, u32[]{:S(2)}) copy-start(f32[512]{0:T(512)} %param.26) | copy-start | bytes 6148
  22.5 2.2 %copy-start.1 = (bf16[512,2048]{1,0:T(8,128)(2,1)S(1)}, bf16[512,2048]{1,0:T(8,128)(2,1)}, u32[]{:S(2)}) copy-start(bf16[512,2048]{1,0:T(8,128)(2,1)} %expand_ref.1) | copy-start | bytes 6291460
  24.6 32.2 %copy-start.8 = (bf16[2048,128]{1,0:T(8,128)(2,1)S(1)}, bf16[2048,128]{1,0:T(8,128)(2,1)}, u32[]{:S(2)}) copy-start(bf16[2048,128]{1,0:T(8,128)(2,1)} %param.29) | copy-start | bytes 1572868
  24.7 32.5 %copy-start.9 = (bf16[128,2048]{1,0:T(8,128)(2,1)S(1)}, bf16[128,2048]{1,0:T(8,128)(2,1)}, u32[]{:S(2)}) copy-start(bf16[128,2048]{1,0:T(8,128)(2,1)} %param.30) | copy-start | bytes 1572868
  24.7 32.8 %copy-start.7 = (bf16[32,32,512]{2,1,0:T(8,128)(2,1)S(1)}, bf16[32,32,512]{2,1,0:T(8,128)(2,1)}, u32[]{:S(2)}) copy-start(bf16[32,32,512]{2,1,0:T(8,128)(2,1)} %param.24) | copy-start | bytes 3145732
  77.8 21.8 %all-to-all-start.2 = ((bf16[32,16,512]{2,1,0:T(8,128)(2,1)}), bf16[32,16,512]{2,1,0:T(8,128)(2,1)S(1)}, u32[]{:S(2)}, u32[]{:S(2)}) async-start(bf16[32,16,512]{2,1,0:T(8,128)(2,1)} %bitcast.35), calls=%async_computation.2 | async-start | bytes 1048576 | tf_op jit(solution)/shard_map/all_to_all | solution.py:443
  99.5 5.6 %copy-start.10 = (bf16[32,16,512]{2,1,0:T(8,128)(2,1)}, bf16[32,16,512]{2,1,0:T(8,128)(2,1)S(1)}, u32[]{:S(2)}) copy-start(bf16[32,16,512]{2,1,0:T(8,128)(2,1)S(1)} %all-to-all-done.2) | copy-start | bytes 1572868
  99.5 21.9 %all-to-all-start = ((bf16[32,16,512]{2,1,0:T(8,128)(2,1)}), bf16[32,16,512]{2,1,0:T(8,128)(2,1)S(1)}, u32[]{:S(2)}, u32[]{:S(2)}) async-start(bf16[32,16,512]{2,1,0:T(8,128)(2,1)} %bitcast.22), calls=%async_computation | async-start | bytes 1048576 | tf_op jit(solution)/shard_map/all_to_all | solution.py:443
  121.4 4.6 %copy-start.11 = (bf16[32,16,512]{2,1,0:T(8,128)(2,1)}, bf16[32,16,512]{2,1,0:T(8,128)(2,1)S(1)}, u32[]{:S(2)}) copy-start(bf16[32,16,512]{2,1,0:T(8,128)(2,1)S(1)} %all-to-all-done) | copy-start | bytes 1572868
  121.4 20.8 %all-to-all-start.3 = ((bf16[32,16,512]{2,1,0:T(8,128)(2,1)}), bf16[32,16,512]{2,1,0:T(8,128)(2,1)S(1)}, u32[]{:S(2)}, u32[]{:S(2)}) async-start(bf16[32,16,512]{2,1,0:T(8,128)(2,1)} %bitcast.85), calls=%async_computation.3 | async-start | bytes 1048576 | tf_op jit(solution)/shard_map/all_to_all | solution.py:445
  142.2 20.8 %all-to-all-start.1 = ((bf16[32,16,512]{2,1,0:T(8,128)(2,1)}), bf16[32,16,512]{2,1,0:T(8,128)(2,1)S(1)}, u32[]{:S(2)}, u32[]{:S(2)}) async-start(bf16[32,16,512]{2,1,0:T(8,128)(2,1)} %bitcast.86), calls=%async_computation.1 | async-start | bytes 1048576 | tf_op jit(solution)/shard_map/all_to_all | solution.py:445
